TPU v7x, 256 devices: a whole 4x4x8 slice. The times are simulated.
256 devices in a mesh: seq: 32 (over z, y), dp: 8 (over x, core).
Axes of the slice: x: 4, y: 4, z: 8, core: 2. Of those that a mesh axis runs over, the one named last changes fastest.
Arguments:
- byte_states: bfloat16 [8, 8192, 4096], P('dp', 'seq'), may hold values from -16 to 16
- byte_patch: int32 [8, 8192], P('dp', 'seq'), may hold values from 0 to 2111, as said below
- patch_owner: int32 [8, 2112], P('dp'), may hold values from 0 to 31, as said below
- qkv_weight: bfloat16 [4096, 3072], P(None, 'dp'), may hold values from -0.09375 to 0.09375
- attention_output_gradient: bfloat16 [8, 2112, 2048], P('dp', 'seq'), may hold values from -6 to 6
Outputs:
- attention: bfloat16 [8, 2112, 2048], P('dp', 'seq')
- state_grad: bfloat16 [8, 8192, 4096], P('dp', 'seq')
- weight_grad: float32 [4096, 3072], P('seq', 'dp')
Inputs may be any that keep to these rules, and one draw needn't show every extreme that they name: `byte_patch`: patch numbers never fall along a sequence, every patch lies within the bytes of one index of seq, and every patch number is used. One index of seq in each sequence, drawn, holds 128 patches of two bytes; every other index holds 64 patches in consecutive pairs that together hold 8 bytes, each patch 1 to 7 bytes. `patch_owner`: patches 0 to 31, 32 to 63 and so on form groups in which every owner appears exactly once.
All inputs are finite; a program needn't handle non-finite values.
Results may differ from a plain program's by a relative error of at most 0.028.
Values may be sent and summed in bfloat16 or wider, within the bound.
A program may use at most 128 MiB of HBM per device.

v0:
```python
import jax
import jax.numpy as jnp
from jax import lax
from jax.sharding import Mesh
from jax.sharding import PartitionSpec as P

QUERY_HEADS = 16
KEY_VALUE_HEADS = 4
HEAD_SIZE = 128
SEQ = ("seq_0", "seq_1")


def gathered_by_axis(shard, axes, dim):
    for axis in reversed(axes):
        shard = lax.all_gather(shard, axis, axis=dim, tiled=True)
    return shard


def sum_by_axis(shard, axes, dim):
    for axis in axes:
        shard = lax.psum_scatter(shard, axis, scatter_dimension=dim, tiled=True)
    return shard


def sum_by_axis_2(terms, axes):
    running = terms.astype(jnp.bfloat16)
    for axis in axes:
        running = lax.psum_scatter(running, axis, scatter_dimension=0, tiled=True)
    return running.astype(jnp.float32)


def in_blocks(shard, dim, peers):
    lengths = shard.shape
    blocks = shard.reshape(*lengths[:dim], peers, lengths[dim] // peers, *lengths[dim + 1 :])
    return jnp.moveaxis(blocks, dim, 0)


def sum_at_owner(shard, axis, dim):
    blocks = in_blocks(shard, dim, lax.axis_size(axis))
    arrived = lax.all_to_all(blocks, axis, split_axis=0, concat_axis=0, tiled=True)
    return arrived.astype(jnp.float32).sum(axis=0)


def contract_rows(left, right):
    return lax.dot_general(
        left, right, (((0,), (0,)), ((), ())), preferred_element_type=jnp.float32
    )


def body(byte_states, byte_patch, patch_owner, qkv_weight, attention_output_gradient):
    seq_count = lax.axis_size(SEQ)
    byte_rows = byte_states[0]
    byte_total = byte_rows.shape[0]
    slot_count = byte_total // 2
    capacity = slot_count // seq_count
    owner_row_list = attention_output_gradient.shape[1]
    patch_ids = byte_patch[0]
    first_patch = patch_ids[0]
    slot_range = jnp.arange(slot_count, dtype=jnp.int32)
    local_ids = patch_ids - first_patch
    onehot = local_ids[None, :] == slot_range[:, None]
    onehot_low = onehot.astype(jnp.bfloat16)
    summed = jnp.dot(onehot_low, byte_rows, preferred_element_type=jnp.float32)
    counts = jnp.sum(onehot.astype(jnp.float32), axis=1)
    pooled = (summed / jnp.maximum(counts, 1.0)[:, None]).astype(jnp.bfloat16)
    padded_owner = jnp.concatenate([patch_owner[0], jnp.zeros((slot_count,), jnp.int32)])
    owners_here = lax.dynamic_slice_in_dim(padded_owner, first_patch, slot_count)
    valid_slot = counts > 0.0
    target_slot = owners_here * capacity + slot_range // seq_count
    send_range = jnp.arange(seq_count * capacity, dtype=jnp.int32)
    routing = (target_slot[None, :] == send_range[:, None]) & valid_slot[None, :]
    routing_low = routing.astype(jnp.bfloat16)
    send_rows = jnp.dot(routing_low, pooled, preferred_element_type=jnp.float32).astype(
        jnp.bfloat16
    )
    send_index = (
        jnp.sum(jnp.where(routing, (first_patch + slot_range)[None, :], 0), axis=1)
        - 1
        + jnp.any(routing, axis=1).astype(jnp.int32)
    )
    recv_rows, recv_index = (
        lax.all_to_all(
            send_rows.reshape(seq_count, capacity, -1), SEQ, split_axis=0, concat_axis=0, tiled=True
        ),
        lax.all_to_all(
            send_index.reshape(seq_count, capacity), SEQ, split_axis=0, concat_axis=0, tiled=True
        ),
    )
    flat_rows = recv_rows.reshape(seq_count * capacity, -1)
    flat_index = recv_index.reshape(-1)
    row_range = jnp.arange(owner_row_list, dtype=jnp.int32)
    collect = (flat_index[None, :] // seq_count == row_range[:, None]) & (flat_index[None, :] >= 0)
    collect_low = collect.astype(jnp.bfloat16)
    own_rows = jnp.dot(collect_low, flat_rows, preferred_element_type=jnp.float32).astype(
        jnp.bfloat16
    )
    own_index = jnp.sum(jnp.where(collect, flat_index[None, :], 0), axis=1)
    all_rows = lax.all_gather(own_rows, "dp", axis=0, tiled=True)
    proj_cols = jnp.dot(all_rows, qkv_weight, preferred_element_type=jnp.float32).astype(
        jnp.bfloat16
    )
    projected_states = lax.all_to_all(proj_cols, "dp", split_axis=0, concat_axis=1, tiled=True)
    query_group_size = QUERY_HEADS // KEY_VALUE_HEADS
    query_row_width = QUERY_HEADS * HEAD_SIZE
    key_row_width = KEY_VALUE_HEADS * HEAD_SIZE
    query_rows = projected_states[:, :query_row_width].reshape(
        owner_row_list, KEY_VALUE_HEADS, query_group_size, HEAD_SIZE
    )
    key_value = projected_states[:, query_row_width:]
    all_pair_list, every_index = (
        gathered_by_axis(key_value, SEQ, 0),
        gathered_by_axis(own_index, SEQ, 0),
    )
    total_patches = all_pair_list.shape[0]
    key_head_count = all_pair_list[:, :key_row_width].reshape(
        total_patches, KEY_VALUE_HEADS, HEAD_SIZE
    )
    value_rows = all_pair_list[:, key_row_width:].reshape(total_patches, KEY_VALUE_HEADS, HEAD_SIZE)
    factor = HEAD_SIZE ** (-0.5)
    scores = (
        jnp.einsum("qhgd,khd->hgqk", query_rows, key_head_count, preferred_element_type=jnp.float32)
        * factor
    )
    allowed = every_index[None, :] <= own_index[:, None]
    scores = jnp.where(allowed[None, None], scores, -jnp.inf)
    row_peak = jnp.max(scores, axis=-1, keepdims=True)
    shifted = jnp.exp(scores - row_peak)
    attend = shifted / jnp.sum(shifted, axis=-1, keepdims=True)
    attended_lower = attend.astype(jnp.bfloat16)
    attended = jnp.einsum(
        "hgqk,khd->qhgd", attended_lower, value_rows, preferred_element_type=jnp.float32
    )
    attn_rows = attended.reshape(owner_row_list, query_row_width).astype(jnp.bfloat16)
    gradient_row_list = attention_output_gradient[0].reshape(
        owner_row_list, KEY_VALUE_HEADS, query_group_size, HEAD_SIZE
    )
    grad_attend = jnp.einsum(
        "qhgd,khd->hgqk", gradient_row_list, value_rows, preferred_element_type=jnp.float32
    )
    row_delta = jnp.einsum("qhgd,qhgd->hgq", gradient_row_list.astype(jnp.float32), attended)
    score_gradient = (attend * (grad_attend - row_delta[..., None])).astype(jnp.bfloat16)
    grad_values = jnp.einsum(
        "hgqk,qhgd->khd", attended_lower, gradient_row_list, preferred_element_type=jnp.float32
    )
    grad_keys = (
        jnp.einsum("hgqk,qhgd->khd", score_gradient, query_rows, preferred_element_type=jnp.float32)
        * factor
    )
    grad_queries = (
        jnp.einsum(
            "hgqk,khd->qhgd", score_gradient, key_head_count, preferred_element_type=jnp.float32
        )
        * factor
    )
    key_terms = jnp.concatenate(
        [
            grad_keys.reshape(total_patches, key_row_width),
            grad_values.reshape(total_patches, key_row_width),
        ],
        axis=1,
    )
    key_grads = sum_by_axis(key_terms.astype(jnp.bfloat16), SEQ, 0).astype(jnp.float32)
    grad_proj = jnp.concatenate(
        [grad_queries.reshape(owner_row_list, query_row_width), key_grads], axis=1
    ).astype(jnp.bfloat16)
    grad_cols = lax.all_to_all(grad_proj, "dp", split_axis=1, concat_axis=0, tiled=True)
    weight_grad = sum_by_axis_2(contract_rows(all_rows, grad_cols), SEQ)
    grad_pooled = sum_at_owner(
        lax.dot_general(
            grad_cols, qkv_weight, (((1,), (1,)), ((), ())), preferred_element_type=jnp.float32
        ).astype(jnp.bfloat16),
        "dp",
        0,
    ).astype(jnp.bfloat16)
    back_rows = contract_rows(collect_low, grad_pooled).astype(jnp.bfloat16)
    returned = lax.all_to_all(
        back_rows.reshape(seq_count, capacity, -1), SEQ, split_axis=0, concat_axis=0, tiled=True
    )
    slot_grads = contract_rows(routing_low, returned.reshape(seq_count * capacity, -1))
    scaled = slot_grads / jnp.maximum(counts, 1.0)[:, None]
    state_grad = lax.dot_general(
        onehot.astype(jnp.float32),
        scaled,
        (((0,), (0,)), ((), ())),
        preferred_element_type=jnp.float32,
    ).astype(jnp.bfloat16)
    return (attn_rows[None], state_grad[None], weight_grad)


def solution(mesh):
    finer = Mesh(mesh.devices.reshape(8, 4, mesh.shape["dp"]), ("seq_0", "seq_1", "dp"))
    placed = (P("dp", SEQ, None), P("dp", SEQ), P("dp", None), P(None, "dp"), P("dp", SEQ, None))
    return jax.shard_map(
        body,
        mesh=finer,
        in_specs=placed,
        out_specs=(P("dp", SEQ, None), P("dp", SEQ, None), P(SEQ, "dp")),
        check_vma=False,
    )
```

profile of v0, /device:TPU:6, one launch (start us, length us, event | category | flops | bytes accessed | tf_op | source)
XLA Modules:
  0.0 499.0 jit_solution(2995310229394458475)
XLA Ops:
  14.3 11.5 %all-to-all-start = ((s32[32,1,4]{2,1,0:T(1,128)}), s32[32,1,4]{2,1,0:T(1,128)S(1)}, u32[]{:S(2)}, u32[]{:S(2)}) async-start(s32[32,1,4]{2,1,0:T(1,128)} %bitcast.4), calls=%async_computation | async-start | bytes 32768 | tf_op jit(solution)/shard_map/all_to_all | solution.py:85
  35.5 5.9 %all-to-all-start.1 = ((bf16[32,4,4096]{2,1,0:T(4,128)(2,1)}), bf16[32,4,4096]{2,1,0:T(4,128)(2,1)}, u32[]{:S(2)}, u32[]{:S(2)}) async-start(bf16[32,4,4096]{2,1,0:T(4,128)(2,1)} %reshape.213), calls=%async_computation.1 | async-start | bytes 2097152 | tf_op jit(solution)/shard_map/all_to_all | solution.py:82
  42.8 26.0 %all-to-all-done.1 = bf16[32,4,4096]{2,1,0:T(4,128)(2,1)} async-done(((bf16[32,4,4096]{2,1,0:T(4,128)(2,1)}), bf16[32,4,4096]{2,1,0:T(4,128)(2,1)}, u32[]{:S(2)}, u32[]{:S(2)}) %all-to-all-start.1) | async-done | bytes 1048608 | tf_op jit(solution)/shard_map/all_to_all | solution.py:82
  73.4 32.1 %all-gather.7.cloned.1.call-done = bf16[8,66,4096]{2,1,0:T(8,128)(2,1)} async-done(((bf16[1,66,4096]{2,1,0:T(8,128)(2,1)}), bf16[8,66,4096]{2,1,0:T(8,128)(2,1)}) %all-gather.7.cloned.1.call-update) | async-done | bytes 4325392 | tf_op jit(solution)/shard_map/all_gather | solution.py:98
  109.8 4.6 convolution_convert_fusion.6
  115.3 13.3 %all_to_all.56 = bf16[8,66,384]{2,1,0:T(8,128)(2,1)S(1)} all-to-all(bf16[8,66,384]{2,1,0:T(8,128)(2,1)} %all_to_all.41), channel_id=1, replica_groups=mesh['seq_0'=8,'seq_1'=4,'dp'=8] {'dp'}, dimensions={0} | all-to-all | bytes 811008 | tf_op jit(solution)/shard_map/all_to_all | solution.py:102
  129.6 14.0 %all-gather.1 = bf16[4,66,1024]{2,1,0:T(8,128)(2,1)} all-gather(bf16[1,66,1024]{2,1,0:T(8,128)(2,1)S(1)} %slice_bitcast_fusion), channel_id=1, replica_groups=mesh['seq_0'=8,'seq_1'=4,'dp'=8] {'seq_1'}, dimensions={0}, use_global_device_ids=true | all-gather | bytes 675840 | tf_op jit(solution)/shard_map/all_gather | solution.py:15
  149.4 8.3 %all-reduce.1 = s32[264]{0:T(512)S(1)} all-reduce(s32[264]{0:T(512)S(1)} %dynamic-update-slice), channel_id=1, replica_groups=mesh['seq_0'=8,'seq_1'=4,'dp'=8] {'seq_1'}, use_global_device_ids=true, to_apply=%add.1 | all-reduce | flops 264 | bytes 2112
  157.9 30.5 %all-reduce.2 = s32[2112]{0:T(1024)S(1)} all-reduce(s32[2112]{0:T(1024)S(1)} %dynamic-update-slice.1), channel_id=1, replica_groups=mesh['seq_0'=8,'seq_1'=4,'dp'=8] {'seq_0'}, use_global_device_ids=true, to_apply=%add.2 | all-reduce | flops 2112 | bytes 16896
  192.0 11.5 %all-gather.5.cloned.1.call-done = bf16[2112,1024]{1,0:T(8,128)(2,1)} async-done(((bf16[264,1024]{1,0:T(8,128)(2,1)}), bf16[2112,1024]{1,0:T(8,128)(2,1)}) %all-gather.5.cloned.1.call-update) | async-done | bytes 4325392 | tf_op jit(solution)/shard_map/all_gather | solution.py:15
  203.4 4.7 fusion.59
  216.2 8.8 %fusion.61 = (f32[4,4,66]{2,1,0:T(4,128)S(1)}, f32[4,4,66,2112]{3,2,1,0:T(8,128)}) fusion(pred[66,2112]{1,0:T(8,128)(4,1)} %broadcast_compare_fusion, bf16[2112,4,128,1]{0,2,3,1:T(8,128)(2,1)} %bitcast.110, bf16[66,4,4,128]{3,2,1,0:T(4,128)(2,1)S(1)} %reshape.217), kind=kOutput, calls=%fused_computation.90 | convolution fusion | flops 579872768 | bytes 11497728 | tf_op jit(solution)/shard_map/sub | solution.py:127
  225.0 5.1 %fusion.16 = bf16[4,4,66,2112]{3,2,1,0:T(8,128)(2,1)S(1)} fusion(f32[4,4,66,2112]{3,2,1,0:T(8,128)} %get-tuple-element.8, f32[4,4,66]{2,1,0:T(4,128)S(1)} %get-tuple-element.7), kind=kLoop, calls=%fused_computation.30 | loop fusion | flops 4460544 | bytes 13385856 | tf_op jit(solution)/shard_map/convert_element_type | solution.py:129
  242.7 6.2 %fusion.3 = bf16[4,4,66,2112]{3,2,1,0:T(8,128)(2,1)S(1)} fusion(bf16[2112,4,128,1]{0,2,3,1:T(8,128)(2,1)} %bitcast.106, f32[4,4,66]{2,1,0:T(4,128)} %copy.109, f32[4,4,66,2112]{3,2,1,0:T(8,128)} %get-tuple-element.8, f32[4,4,66]{2,1,0:T(4,128)} %copy-done.7, bf16[66,4,4,128]{3,2,1,0:T(4,128)(2,1)} %reshape_squeeze.3), kind=kOutput, calls=%fused_computation.3 | convolution fusion | flops 579870720 | bytes 15823104 | tf_op jit(solution)/shard_map/qhgd,khd->hgqk/dot_general | solution.py:137
  258.9 4.7 pad_maximum_fusion
  263.6 6.4 %copy.123 = bf16[2112,1024]{1,0:T(8,128)(2,1)} copy(bf16[2112,1024]{0,1:T(8,128)(2,1)} %pad_maximum_fusion) | data formatting | bytes 8650752
  270.6 54.5 %reduce-scatter.12.cloned.1.call-done = bf16[264,1024]{1,0:T(8,128)(2,1)} async-done(((bf16[2112,1024]{1,0:T(8,128)(2,1)}), bf16[264,1024]{1,0:T(8,128)(2,1)}) %reduce-scatter.12.cloned.1.call-update) | async-done | bytes 540688 | tf_op jit(solution)/shard_map/reduce_scatter | solution.py:21
  325.2 14.7 %fusion = bf16[72,1024]{1,0:T(8,128)(2,1)S(1)} fusion(bf16[264,1024]{1,0:T(8,128)(2,1)} %reduce-scatter.12.cloned.1.call-done), kind=kCustom, calls=%all-reduce-scatter | all-reduce-scatter fusion | flops 294913 | bytes 689152
  343.7 4.7 fusion.23
  353.8 12.1 %all_to_all.57 = bf16[66,8,384]{2,0,1:T(8,128)(2,1)} all-to-all(bf16[66,8,384]{2,0,1:T(8,128)(2,1)S(1)} %copy.99), channel_id=1, replica_groups=mesh['seq_0'=8,'seq_1'=4,'dp'=8] {'dp'}, dimensions={1} | all-to-all | bytes 811008 | tf_op jit(solution)/shard_map/all_to_all | solution.py:166
  367.0 7.1 %convolution_convert_fusion.1 = bf16[4096,384]{1,0:T(8,128)(2,1)} fusion(bf16[528,4096]{1,0:T(8,128)(2,1)} %reshape.231, bf16[528,384]{1,0:T(8,128)(2,1)S(1)} %all_to_all.47), kind=kOutput, calls=%fused_computation.8 | convolution fusion | flops 1662517248 | bytes 7876608 | tf_op jit(solution)/shard_map/dot_general | solution.py:45
  382.9 60.6 %all_to_all.58 = bf16[8,66,4096]{2,1,0:T(8,128)(2,1)} all-to-all(bf16[8,66,4096]{2,1,0:T(8,128)(2,1)} %reshape.221), channel_id=1, replica_groups=mesh['seq_0'=8,'seq_1'=4,'dp'=8] {'dp'}, dimensions={0} | all-to-all | bytes 8650752 | tf_op jit(solution)/shard_map/all_to_all | solution.py:40
  452.4 5.1 %all-to-all-start.5 = ((bf16[32,4,4096]{2,1,0:T(4,128)(2,1)}), bf16[32,4,4096]{2,1,0:T(4,128)(2,1)}, u32[]{:S(2)}, u32[]{:S(2)}) async-start(bf16[32,4,4096]{2,1,0:T(4,128)(2,1)} %reshape.222), calls=%async_computation.5 | async-start | bytes 2097152 | tf_op jit(solution)/shard_map/all_to_all | solution.py:176
  460.2 25.0 %all-to-all-done.5 = bf16[32,4,4096]{2,1,0:T(4,128)(2,1)} async-done(((bf16[32,4,4096]{2,1,0:T(4,128)(2,1)}), bf16[32,4,4096]{2,1,0:T(4,128)(2,1)}, u32[]{:S(2)}, u32[]{:S(2)}) %all-to-all-start.5) | async-done | bytes 1048608 | tf_op jit(solution)/shard_map/all_to_all | solution.py:176
  (128 shorter events, 103.8 us)
Async XLA Ops:
  7.2 102.6 %copy-start = (bf16[4096,384]{1,0:T(8,128)(2,1)S(1)}, bf16[4096,384]{1,0:T(8,128)(2,1)}, u32[]{:S(2)}) copy-start(bf16[4096,384]{1,0:T(8,128)(2,1)} %param.8) | copy-start | bytes 9437188
  9.8 19.3 %copy-start.15 = (s32[1,256]{1,0:T(1,128)}, s32[1,256]{1,0:T(1,128)S(1)}, u32[]{:S(2)}) copy-start(s32[1,256]{1,0:T(1,128)S(1)} %broadcast_subtract_fusion) | copy-start | bytes 3076
  11.2 17.9 %copy-start.18 = (pred[128]{0:T(512)(128)(4,1)}, pred[128]{0:T(512)(128)(4,1)S(1)}, u32[]{:S(2)}) copy-start(pred[128]{0:T(512)(128)(4,1)S(1)} %broadcast_compare_fusion.1) | copy-start | bytes 388
  13.4 15.8 %copy-start.11 = (s32[128]{0:T(128)}, s32[128]{0:T(128)S(1)}, u32[]{:S(2)}) copy-start(s32[128]{0:T(128)S(1)} %get-tuple-element.9) | copy-start | bytes 1540
  14.3 21.2 %all-to-all-start = ((s32[32,1,4]{2,1,0:T(1,128)}), s32[32,1,4]{2,1,0:T(1,128)S(1)}, u32[]{:S(2)}, u32[]{:S(2)}) async-start(s32[32,1,4]{2,1,0:T(1,128)} %bitcast.4), calls=%async_computation | async-start | bytes 32768 | tf_op jit(solution)/shard_map/all_to_all | solution.py:85
  35.5 33.3 %all-to-all-start.1 = ((bf16[32,4,4096]{2,1,0:T(4,128)(2,1)}), bf16[32,4,4096]{2,1,0:T(4,128)(2,1)}, u32[]{:S(2)}, u32[]{:S(2)}) async-start(bf16[32,4,4096]{2,1,0:T(4,128)(2,1)} %reshape.213), calls=%async_computation.1 | async-start | bytes 2097152 | tf_op jit(solution)/shard_map/all_to_all | solution.py:82
  41.3 64.1 %all-gather.7.cloned.1.call-start = ((), (), s32[]{:S(2)}) async-start(), calls=%async_computation.12 | async-start | bytes 5308416 | tf_op jit(solution)/shard_map/all_gather | solution.py:98
  42.7 62.8 %copy-start.13 = (s32[128]{0:T(128)}, s32[128]{0:T(128)S(1)}, u32[]{:S(2)}) copy-start(s32[128]{0:T(128)S(1)} %broadcast_in_dim_reshape.2) | copy-start | bytes 1540
  42.7 62.7 %copy-start.8 = (pred[128]{0:T(512)(128)(4,1)}, pred[128]{0:T(512)(128)(4,1)S(1)}, u32[]{:S(2)}) copy-start(pred[128]{0:T(512)(128)(4,1)S(1)} %broadcast_compare_fusion.2) | copy-start | bytes 388
  73.3 130.1 %all-gather.5.cloned.1.call-start = ((), (), s32[]{:S(2)}) async-start(), calls=%async_computation.9 | async-start | bytes 4866048 | tf_op jit(solution)/shard_map/all_gather | solution.py:15
  115.3 30.4 %copy-start.6 = (bf16[1,66,2048]{2,1,0:T(8,128)(2,1)S(1)}, bf16[1,66,2048]{2,1,0:T(8,128)(2,1)}, u32[]{:S(2)}) copy-start(bf16[1,66,2048]{2,1,0:T(8,128)(2,1)} %param.9) | copy-start | bytes 811012
  115.3 31.2 %copy-start.20 = (u32[256]{0:T(256)S(1)}, u32[256]{0:T(256)}, u32[]{:S(2)}) copy-start(u32[256]{0:T(256)} %constant.64) | copy-start | bytes 3076
  115.3 32.5 %copy-start.17 = (u32[256]{0:T(256)S(1)}, u32[256]{0:T(256)}, u32[]{:S(2)}) copy-start(u32[256]{0:T(256)} %constant.59) | copy-start | bytes 3076
  115.3 33.7 %copy-start.9 = (pred[128]{0:T(512)(128)(4,1)S(1)}, pred[128]{0:T(512)(128)(4,1)}, u32[]{:S(2)}) copy-start(pred[128]{0:T(512)(128)(4,1)} %copy-done.8) | copy-start | bytes 388
  115.3 33.7 %copy-start.14 = (s32[128]{0:T(128)S(1)}, s32[128]{0:T(128)}, u32[]{:S(2)}) copy-start(s32[128]{0:T(128)} %copy-done.13) | copy-start | bytes 1540
  145.6 179.6 %reduce-scatter.12.cloned.1.call-start = ((), (), s32[]{:S(2)}) async-start(), calls=%async_computation.13 | async-start | bytes 4866048 | tf_op jit(solution)/shard_map/reduce_scatter | solution.py:21
  270.0 187.6 %reduce-scatter.8.cloned.1.call-start = ((), (), s32[]{:S(2)}) async-start(), calls=%async_computation.10 | async-start | bytes 3538944 | tf_op jit(solution)/shard_map/reduce_scatter | solution.py:28
  339.9 10.4 %collective-permute-start = (bf16[18,1024]{1,0:T(8,128)(2,1)S(1)}, bf16[18,1024]{1,0:T(8,128)(2,1)S(1)}, u32[]{:S(2)}, u32[]{:S(2)}) collective-permute-start(bf16[18,1024]{1,0:T(8,128)(2,1)S(1)} %slice.25), channel_id=1, source_target_pairs={{0,8},{8,16},{16,24},{1,9},{9,17},{17,25},{2,10},{10,18},{18,26},{... | collective-permute-start | bytes 110600
  450.2 37.1 %copy-start.12 = (s32[128]{0:T(128)S(1)}, s32[128]{0:T(128)}, u32[]{:S(2)}) copy-start(s32[128]{0:T(128)} %copy-done.11) | copy-start | bytes 1540
  450.2 37.1 %copy-start.16 = (s32[1,256]{1,0:T(1,128)S(1)}, s32[1,256]{1,0:T(1,128)}, u32[]{:S(2)}) copy-start(s32[1,256]{1,0:T(1,128)} %copy-done.15) | copy-start | bytes 3076
  450.2 37.1 %copy-start.19 = (pred[128]{0:T(512)(128)(4,1)S(1)}, pred[128]{0:T(512)(128)(4,1)}, u32[]{:S(2)}) copy-start(pred[128]{0:T(512)(128)(4,1)} %copy-done.18) | copy-start | bytes 388
  450.2 37.1 %copy-start.22 = (f32[128]{0:T(128)S(1)}, f32[128]{0:T(128)}, u32[]{:S(2)}) copy-start(f32[128]{0:T(128)} %copy-done.21) | copy-start | bytes 1540
  452.4 32.8 %all-to-all-start.5 = ((bf16[32,4,4096]{2,1,0:T(4,128)(2,1)}), bf16[32,4,4096]{2,1,0:T(4,128)(2,1)}, u32[]{:S(2)}, u32[]{:S(2)}) async-start(bf16[32,4,4096]{2,1,0:T(4,128)(2,1)} %reshape.222), calls=%async_computation.5 | async-start | bytes 2097152 | tf_op jit(solution)/shard_map/all_to_all | solution.py:176
  457.5 33.4 %reduce-scatter.10.cloned.1.call-start = ((), (), s32[]{:S(2)}) async-start(), calls=%async_computation.11 | async-start | bytes 491520 | tf_op jit(solution)/shard_map/reduce_scatter | solution.py:28
  (8 other events, 31.7 us)
Sparse Core Ops, SparseCore 0:
  73.4 31.9 all-gather.6
  145.7 57.6 all-gather.4
  270.1 54.9 reduce-scatter.11
  374.2 43.0 reduce-scatter.7
  460.7 25.5 reduce-scatter.9
where the time goes:
time: 503 us; the launch traced here: 499 us
  waiting for transfers between devices  154 us (31%)
  blocking collectives  153 us (30%)
  local copies, waits for them, and re-layouts  68.2 us (14%)
  matrix products  57.3 us (11%)
  starting transfers between devices  26.4 us (5%)
  other arithmetic  21.8 us (4%)
  between operations  18 us (4%)
    all_to_all x1, blocking collectives, sum_at_owner(): lax.all_to_all(blocks, axis, split_axis=0, concat_axis=0, tiled=True)  60.6 us
    reduce_scatter x1, waiting for transfers between devices, sum_by_axis(): shard = lax.psum_scatter(shard, axis, scatter_dimension=dim, tiled=True)  54.5 us
    unnamed x3, blocking collectives  53.5 us
    all_gather x1, waiting for transfers between devices, body(): all_rows = lax.all_gather(own_rows, 'dp', axis=0, tiled=True)  32.1 us
    all_to_all x1, waiting for transfers between devices, body(): lax.all_to_all(send_rows.reshape(seq_count, capacity, -1), SEQ, split_axi...  26 us
    all_to_all x1, waiting for transfers between devices, body(): lax.all_to_all(back_rows.reshape(seq_count, capacity, -1), SEQ, split_axi...  25 us
    unnamed x62, local copies, waits for them, and re-layouts  20.9 us
    all_gather x1, blocking collectives, gathered_by_axis(): shard = lax.all_gather(shard, axis, axis=dim, tiled=True)  14 us
  transfers between devices with their start and end apart: 9, of which 6 were waited for; matrix products, arithmetic and copies ran while one was open for 9% of the time, Pallas kernels for 0%

commit v1 on v0

v1 whole, which is shorter than its diff:
```python
import functools

import jax
import jax.numpy as jnp
from jax import lax
from jax.experimental import pallas as pl
from jax.experimental.pallas import tpu as pltpu
from jax.sharding import Mesh
from jax.sharding import PartitionSpec as P

QUERY_HEADS = 16
KEY_VALUE_HEADS = 4
HEAD = 128
FACTOR = HEAD ** (-0.5)
NZ, NY, NX, NC = 8, 4, 4, 2
NS, NDP = NZ * NY, NX * NC
SEQ = ("z", "y")
DP = ("x", "c")
MAIN = 64
BYTES = 256
DG = 4096
PATCHES = 2112
COLS = 384
BF = jnp.bfloat16
F32 = jnp.float32
VMEM_LIMIT = 56 << 20


def dot(a, b):
    return jnp.dot(a, b, preferred_element_type=F32)


def dot_t(a, b):
    return lax.dot_general(a, b, (((0,), (0,)), ((), ())), preferred_element_type=F32)


def pool_kernel(
    ids_ref, owner_ref, states_ref, grad_ref,
    main_ref, over_ref, slot_ref, flag_ref, band_ref,
    onehot_ref,
):
    s = lax.axis_index("z") * NY + lax.axis_index("y")

    @pl.when(pl.program_id(0) == 0)
    def _():
        ids = ids_ref[...]
        first = jnp.min(ids, axis=1, keepdims=True)
        last = jnp.max(ids, axis=1, keepdims=True)
        group = (ids - first) >> 5
        patch = lax.broadcasted_iota(jnp.int32, (PATCHES, BYTES), 0)
        hit = jnp.where(patch == ids, 1.0, 0.0).astype(BF)
        owner = jnp.broadcast_to(owner_ref[...].astype(F32), (16, PATCHES)).astype(BF)
        byte_owner = dot(owner, hit)[0:1].astype(jnp.int32)
        over = MAIN + (byte_owner & 3) * 16 + (byte_owner >> 2) * 2 + (group - 2)
        slot = jnp.where(group < 2, group * 32 + byte_owner, over)
        slot_ref[...] = slot
        rows = lax.broadcasted_iota(jnp.int32, (2 * MAIN, BYTES), 0)
        onehot_ref[...] = jnp.where(rows == slot, 1.0, 0.0)
        spike = jnp.where(last - first >= MAIN, s.astype(F32), 0.0)
        flag_ref[...] = jnp.broadcast_to(spike, (8, 128))

    onehot = onehot_ref[...]
    counts = jnp.maximum(jnp.sum(onehot, axis=1, keepdims=True), 1.0)
    pooled = (dot(onehot.astype(BF), states_ref[0]) / counts).astype(BF)
    main_ref[...] = pooled[:MAIN]
    over_ref[...] = pooled[MAIN:].reshape(NY, 16, pooled.shape[1])
    grad = grad_ref[0]
    for z in range(NZ - 1):
        band_ref[z] = grad[8 * z : 8 * z + 16]
    band_ref[NZ - 1] = jnp.zeros_like(band_ref[NZ - 1])
    band_ref[NZ - 1, 0:10, :] = grad[56:66]


def pool(byte_patch, patch_owner, byte_states, grad):
    steps = 4
    width = DG // steps
    return pl.pallas_call(
        pool_kernel,
        grid=(steps,),
        in_specs=[
            pl.BlockSpec((1, BYTES), lambda i: (0, 0)),
            pl.BlockSpec((1, PATCHES), lambda i: (0, 0)),
            pl.BlockSpec((1, BYTES, width), lambda i: (0, 0, i)),
            pl.BlockSpec((1, 66, 512), lambda i: (0, 0, i)),
        ],
        out_specs=[
            pl.BlockSpec((MAIN, width), lambda i: (0, i)),
            pl.BlockSpec((NY, 16, width), lambda i: (0, 0, i)),
            pl.BlockSpec((1, BYTES), lambda i: (0, 0)),
            pl.BlockSpec((8, 128), lambda i: (0, 0)),
            pl.BlockSpec((NZ, 16, 512), lambda i: (0, 0, i)),
        ],
        out_shape=[
            jax.ShapeDtypeStruct((MAIN, DG), BF),
            jax.ShapeDtypeStruct((NY, 16, DG), BF),
            jax.ShapeDtypeStruct((1, BYTES), jnp.int32),
            jax.ShapeDtypeStruct((8, 128), F32),
            jax.ShapeDtypeStruct((NZ, 16, 2048), BF),
        ],
        scratch_shapes=[pltpu.VMEM((2 * MAIN, BYTES), F32)],
        name="pool",
    )(byte_patch, patch_owner, byte_states, grad)


MESH = pl.DeviceIdType.MESH
ANY = pl.BlockSpec(memory_space=pl.ANY)
VM = pl.BlockSpec(memory_space=pltpu.VMEM)


def here():
    return [lax.axis_index(name) for name in ("z", "y", "x", "c")]


def send(src, dst, pair, **device):
    return pltpu.make_async_remote_copy(
        src_ref=src, dst_ref=dst, send_sem=pair[0], recv_sem=pair[1],
        device_id=device, device_id_type=MESH,
    )


def greet(devices):
    barrier = pltpu.get_barrier_semaphore()
    for device in devices:
        pl.semaphore_signal(barrier, inc=1, device_id=device, device_id_type=MESH)
    pl.semaphore_wait(barrier, len(devices))


def gather_kernel(
    main, over, flag, band,
    all_main, all_over, spot, gy, gz,
    ybuf, zsrc, zbuf, mine, fy, fsum, fz,
    local, main_s, main_r, ys, yr, zs, zr, os_, or_,
):
    z, y, x, c = here()
    n = x * 2 + c
    ys_at = [lax.rem(y + j, NY) for j in range(NY)]
    zs_at = [lax.rem(z + j, NZ) for j in range(NZ)]
    dp_at = [lax.rem(n + j, NDP) for j in range(NDP)]
    right, left, other = lax.rem(x + 1, NX), lax.rem(x + 3, NX), 1 - c
    greet(
        [{"y": ys_at[j]} for j in range(1, NY)]
        + [{"z": zs_at[j]} for j in range(1, NZ)]
        + [{"x": p // 2, "c": lax.rem(p, 2)} for p in dp_at[1:]]
    )

    def half(block, i):
        return block.at[pl.ds(32 * i, 32), :]

    def pair(i):
        return main_s.at[i], main_r.at[i]

    mine_out = all_main.at[n]
    first = [
        send(main, mine_out, pair(1), x=right),
        send(main, mine_out, pair(2), x=left),
        send(main, mine_out, pair(0), c=other),
    ]
    for copy in first:
        copy.start()
    keep = [pltpu.make_async_copy(main, mine_out, local.at[0])]

    stage_y = []
    for j in range(1, NY):
        stage_y.append(send(over.at[ys_at[j]], ybuf.at[y], (ys.at[0, j], yr.at[0, j]), y=ys_at[j]))
        stage_y.append(send(flag, fy.at[y], (ys.at[1, j], yr.at[1, j]), y=ys_at[j]))
    here_y = [
        pltpu.make_async_copy(over.at[y], ybuf.at[y], local.at[1]),
        pltpu.make_async_copy(flag, fy.at[y], local.at[2]),
    ]
    for copy in stage_y + here_y + keep:
        copy.start()

    def columns(h):
        return pl.ds(pl.multiple_of(h * 512, 512), 512)

    grads_y = [
        send(band.at[:, :, columns(ys_at[j])], gy.at[y], (ys.at[2, j], yr.at[2, j]), y=ys_at[j])
        for j in range(1, NY)
    ]
    keep_y = pltpu.make_async_copy(band.at[:, :, columns(y)], gy.at[y], local.at[3])
    for copy in grads_y + [keep_y]:
        copy.start()

    for copy in stage_y:
        copy.wait_recv()
    for copy in here_y:
        copy.wait()
    rows = (
        ybuf[0].astype(F32) + ybuf[1].astype(F32) + ybuf[2].astype(F32) + ybuf[3].astype(F32)
    ).astype(BF)
    for k in range(NZ):
        zsrc[k] = rows[2 * k : 2 * k + 2]
    fsum[...] = fy[0] + fy[1] + fy[2] + fy[3]
    stage_z = []
    for j in range(1, NZ):
        stage_z.append(send(zsrc.at[zs_at[j]], zbuf.at[z], (zs.at[0, j], zr.at[0, j]), z=zs_at[j]))
        stage_z.append(send(fsum, fz.at[z], (zs.at[1, j], zr.at[1, j]), z=zs_at[j]))
    here_z = [
        pltpu.make_async_copy(zsrc.at[z], zbuf.at[z], local.at[4]),
        pltpu.make_async_copy(fsum, fz.at[z], local.at[5]),
    ]
    for copy in stage_z + here_z:
        copy.start()
    for copy in stage_z:
        copy.wait_recv()
    for copy in here_z:
        copy.wait()
    total = zbuf[0].astype(F32)
    found = fz[0]
    for k in range(1, NZ):
        total = total + zbuf[k].astype(F32)
        found = found + fz[k]
    mine[...] = total.astype(BF)
    spot[...] = found
    overs = [
        send(mine, all_over.at[n], (os_.at[j], or_.at[j]), x=dp_at[j] // 2, c=lax.rem(dp_at[j], 2))
        for j in range(1, NDP)
    ]
    keep_o = pltpu.make_async_copy(mine, all_over.at[n], local.at[6])
    for copy in overs + [keep_o]:
        copy.start()

    for copy in grads_y:
        copy.wait_recv()
    keep_y.wait()
    grads_z = [
        send(gy.at[:, zs_at[j]], gz.at[z], (zs.at[2, j], zr.at[2, j]), z=zs_at[j])
        for j in range(1, NZ)
    ]
    keep_z = pltpu.make_async_copy(gy.at[:, z], gz.at[z], local.at[7])
    for copy in grads_z + [keep_z]:
        copy.start()

    from_left = all_main.at[left * 2 + c]
    from_right = all_main.at[right * 2 + c]
    far = all_main.at[lax.rem(x + 2, NX) * 2 + c]
    first[0].wait_recv()
    on_right = send(half(from_left, 0), half(from_left, 0), pair(3), x=right)
    side_left = send(from_left, from_left, pair(5), c=other)
    on_right.start()
    first[1].wait_recv()
    on_left = send(half(from_right, 1), half(from_right, 1), pair(4), x=left)
    side_right = send(from_right, from_right, pair(6), c=other)
    on_left.start()
    side_left.start()
    side_right.start()
    on_right.wait_recv()
    side_a = send(half(far, 0), half(far, 0), pair(7), c=other)
    side_a.start()
    on_left.wait_recv()
    side_b = send(half(far, 1), half(far, 1), pair(8), c=other)
    side_b.start()
    first[2].wait_recv()
    for copy in (side_left, side_right, side_a, side_b, *overs, *grads_z):
        copy.wait_recv()
    for copy in (
        *first, on_right, on_left, side_left, side_right, side_a, side_b,
        *stage_y, *stage_z, *overs, *grads_y, *grads_z,
    ):
        copy.wait_send()
    for copy in (*keep, keep_o, keep_z):
        copy.wait()


def gather_rows(main, over, flag, band):
    dma = pltpu.SemaphoreType.DMA
    return pl.pallas_call(
        gather_kernel,
        in_specs=[ANY, ANY, VM, ANY],
        out_specs=[ANY, ANY, VM, ANY, ANY],
        out_shape=[
            jax.ShapeDtypeStruct((NDP, MAIN, DG), BF),
            jax.ShapeDtypeStruct((NDP, 2, DG), BF),
            jax.ShapeDtypeStruct((8, 128), F32),
            jax.ShapeDtypeStruct((NY, NZ, 16, 512), BF),
            jax.ShapeDtypeStruct((NZ, NY, 16, 512), BF),
        ],
        scratch_shapes=[
            pltpu.VMEM((NY, 16, DG), BF),
            pltpu.VMEM((NZ, 2, DG), BF),
            pltpu.VMEM((NZ, 2, DG), BF),
            pltpu.VMEM((2, DG), BF),
            pltpu.VMEM((NY, 8, 128), F32),
            pltpu.VMEM((8, 128), F32),
            pltpu.VMEM((NZ, 8, 128), F32),
            dma((8,)),
            dma((9,)),
            dma((9,)),
            dma((3, NY)),
            dma((3, NY)),
            dma((3, NZ)),
            dma((3, NZ)),
            dma((NDP,)),
            dma((NDP,)),
        ],
        compiler_params=pltpu.CompilerParams(
            collective_id=0, has_side_effects=True, vmem_limit_bytes=VMEM_LIMIT
        ),
        name="gather_rows",
    )(main, over, flag, band)


def spread_kernel(slot_ref, pooled_ref, over_ref, am_ref, ao_ref, spot_ref, out_ref, att_ref, rows_ref):
    slot = slot_ref[...]
    rows = lax.broadcasted_iota(jnp.int32, (2 * MAIN, BYTES), 0)
    onehot = jnp.where(rows == slot, 1.0, 0.0)
    counts = jnp.broadcast_to(jnp.sum(onehot, axis=1, keepdims=True), (2 * MAIN, 128))
    low = onehot.astype(BF)
    byte_count = jnp.maximum(dot_t(low, counts.astype(BF))[:, 0:1], 1.0)
    rows_ref[0:MAIN, :] = pooled_ref[0:MAIN, :]
    for j in range(NY):
        for k in range(NZ):
            at = MAIN + j * 16 + k * 2
            rows_ref[at : at + 2, :] = over_ref[j, k]
    out_ref[0] = (dot_t(low, rows_ref[...]) / byte_count).astype(BF)

    edge = 2 * spot_ref[0:1, 0:1].astype(jnp.int32) + 2
    row = lax.broadcasted_iota(jnp.int32, (66, 64), 0)
    col = lax.broadcasted_iota(jnp.int32, (66, 64), 1)
    keep = ((row < edge) & (col == row)) | ((row > edge + 1) & (col == row - 2))
    att = dot(jnp.where(keep, 1.0, 0.0).astype(BF), am_ref[0].reshape(64, 512))
    row = lax.broadcasted_iota(jnp.int32, (66, 16), 0)
    col = lax.broadcasted_iota(jnp.int32, (66, 16), 1)
    keep = (col == row - edge) & (col < 2)
    extra = jnp.concatenate([ao_ref[0], jnp.zeros((8, 512), BF)], axis=0)
    att = att + dot(jnp.where(keep, 1.0, 0.0).astype(BF), extra)
    att_ref[0] = att.astype(BF)


def spread(slot, pooled, over, am, ao, spot):
    steps = 4
    width = DG // steps
    return pl.pallas_call(
        spread_kernel,
        grid=(steps,),
        in_specs=[
            pl.BlockSpec((1, BYTES), lambda i: (0, 0)),
            pl.BlockSpec((72, width), lambda i: (0, i)),
            pl.BlockSpec((NY, NZ, 2, width), lambda i: (0, 0, 0, i)),
            pl.BlockSpec((1, NZ, 8, 512), lambda i: (i, 0, 0, 0)),
            pl.BlockSpec((1, 8, 512), lambda i: (i, 0, 0)),
            pl.BlockSpec((8, 128), lambda i: (0, 0)),
        ],
        out_specs=[
            pl.BlockSpec((1, BYTES, width), lambda i: (0, 0, i)),
            pl.BlockSpec((1, 66, 512), lambda i: (0, 0, i)),
        ],
        out_shape=[
            jax.ShapeDtypeStruct((1, BYTES, DG), BF),
            jax.ShapeDtypeStruct((1, 66, 2048), BF),
        ],
        scratch_shapes=[pltpu.VMEM((2 * MAIN, width), BF)],
        name="spread",
    )(slot, pooled, over, am, ao, spot)


ROWS = 72
OVER = 2


def project_kernel(main_ref, over_ref, weight_ref, out_ref, acc, acc_over, over_rows):
    step = pl.program_id(0)

    @pl.when(step == 0)
    def _():
        acc[...] = jnp.zeros_like(acc)
        acc_over[...] = jnp.zeros_like(acc_over)

    for n in range(NDP):
        over_rows[2 * n : 2 * n + 2, :] = over_ref[n]
    weight = weight_ref[...]
    acc[...] += dot(main_ref[...].reshape(NDP * MAIN, weight.shape[0]), weight)
    acc_over[...] += dot(over_rows[...], weight)

    @pl.when(step == pl.num_programs(0) - 1)
    def _():
        total = acc[...].astype(BF)
        extra = acc_over[...].astype(BF)
        for n in range(NDP):
            out_ref[n, 0:MAIN, :] = total[MAIN * n : MAIN * (n + 1)]
            out_ref[n, MAIN:ROWS, :] = jnp.zeros((ROWS - MAIN, COLS), BF)
            out_ref[n, MAIN : MAIN + 2, :] = extra[2 * n : 2 * n + 2]


def project(all_main, all_over, weight):
    steps = 4
    depth = DG // steps
    return pl.pallas_call(
        project_kernel,
        grid=(steps,),
        in_specs=[
            pl.BlockSpec((NDP, MAIN, depth), lambda i: (0, 0, i)),
            pl.BlockSpec((NDP, 2, depth), lambda i: (0, 0, i)),
            pl.BlockSpec((depth, COLS), lambda i: (i, 0)),
        ],
        out_specs=pl.BlockSpec((NDP, ROWS, COLS), lambda i: (0, 0, 0)),
        out_shape=jax.ShapeDtypeStruct((NDP, ROWS, COLS), BF),
        scratch_shapes=[
            pltpu.VMEM((NDP * MAIN, COLS), F32),
            pltpu.VMEM((16, COLS), F32),
            pltpu.VMEM((16, depth), BF),
        ],
        compiler_params=pltpu.CompilerParams(vmem_limit_bytes=VMEM_LIMIT),
        name="project",
    )(all_main, all_over, weight)


def lanes(i):
    return pl.ds(pl.multiple_of(i * HEAD, HEAD), HEAD)


def heads_kernel(proj, heads, kv, local, hs, hr, rs, rr, ls, lr):
    z, y, x, c = here()
    n = x * 2 + c
    up, down = lax.rem(z + 1, NZ), lax.rem(z + NZ - 1, NZ)
    peers = []
    for j in range(NDP * NY):
        if j:
            p, q = lax.rem(n + j // NY, NDP), lax.rem(y + j, NY)
            peers.append({"y": q, "x": p // 2, "c": lax.rem(p, 2)})
    greet(peers + [{"z": up}, {"z": down}])

    def plan(j, i):
        p = lax.rem(n + j, NDP)
        head = n * 3 + i
        query = head < QUERY_HEADS
        slot = jnp.where(query, lax.rem(head, 4), head // 4)
        target = jnp.where(query, head // 4, lax.rem(head, 4))
        src = proj.at[p, :, i * HEAD : (i + 1) * HEAD]
        dst = heads.at[slot, y]
        there = send(
            src, dst, (hs.at[j, i], hr.at[slot, y]), y=target, x=p // 2, c=lax.rem(p, 2)
        )
        stay = pltpu.make_async_copy(src, dst, hr.at[slot, y])
        own = target == y
        return there, stay, own

    for i in (2, 1, 0):
        for j in range(1, NDP):
            plan(j, i)[0].start()
        there, stay, own = plan(0, i)

        @pl.when(own)
        def _():
            stay.start()

        @pl.when(jnp.logical_not(own))
        def _():
            there.start()

    def arrived(slot, k):
        pltpu.make_async_copy(heads.at[slot, k], heads.at[slot, k], hr.at[slot, k]).wait()

    ups, downs, keeps = [], [], []
    for t in range(1, 5):
        for i in range(2):
            if t == 1:
                for k in range(NY):
                    arrived(4 + i, k)
                keep = pltpu.make_async_copy(heads.at[4 + i], kv.at[i, z], local.at[i])
                keep.start()
                keeps.append(keep)
                above = below = heads.at[4 + i]
            else:
                ups[2 * (t - 2) + i].wait_recv()
                downs[2 * (t - 2) + i].wait_recv()
                above = kv.at[i, lax.rem(z + NZ - (t - 1), NZ)]
                below = kv.at[i, lax.rem(z + (t - 1), NZ)]
            copy = send(above, kv.at[i, lax.rem(z + NZ - (t - 1), NZ)], (rs.at[t - 1, i], rr.at[t - 1, i]), z=up)
            copy.start()
            ups.append(copy)
            if t < 4:
                copy = send(below, kv.at[i, lax.rem(z + (t - 1), NZ)], (ls.at[t - 1, i], lr.at[t - 1, i]), z=down)
                copy.start()
                downs.append(copy)
    for slot in range(4):
        for k in range(NY):
            arrived(slot, k)
    for i in range(2):
        ups[6 + i].wait_recv()
    for copy in ups + downs:
        copy.wait_send()
    for copy in keeps:
        copy.wait()
    for i in range(3):
        for j in range(1, NDP):
            plan(j, i)[0].wait_send()
        there, stay, own = plan(0, i)

        @pl.when(jnp.logical_not(own))
        def _():
            there.wait_send()


def to_heads(proj):
    dma = pltpu.SemaphoreType.DMA
    return pl.pallas_call(
        heads_kernel,
        in_specs=[ANY],
        out_specs=[ANY, ANY],
        out_shape=[
            jax.ShapeDtypeStruct((6, NY, ROWS, HEAD), BF),
            jax.ShapeDtypeStruct((2, NZ, NY, ROWS, HEAD), BF),
        ],
        scratch_shapes=[
            dma((2,)),
            dma((NDP, 3)),
            dma((6, NY)),
            dma((4, 2)),
            dma((4, 2)),
            dma((3, 2)),
            dma((3, 2)),
        ],
        compiler_params=pltpu.CompilerParams(collective_id=1, has_side_effects=True),
        name="to_heads",
    )(proj)


CHUNK = 352
QM = 256
QO = 32
KM = NS * MAIN


def attention_kernel(
    heads_ref, kv_ref, gy_ref, gz_ref, spot_ref, kidx_ref, qidx_ref, qoidx_ref,
    om_ref, oo_ref, dq_ref, dkv_ref,
    k_ref, v_ref, kt, vt, g_ref, qo_ref, go_ref, scores, dk, dv,
):
    chunks = PATCHES // CHUNK
    z = lax.axis_index("z")
    spot = spot_ref[0:1, 0:1].astype(jnp.int32)

    for i, ref in enumerate((k_ref, v_ref)):
        for k in range(NZ):
            ref[k * QM : (k + 1) * QM, :] = kv_ref[i, k, :, 0:MAIN, :].reshape(QM, HEAD)
            for j in range(NY):
                at = KM + 2 * (k * NY + j)
                ref[at : at + 2, :] = kv_ref[i, k, j, MAIN : MAIN + 2, :]
    kt[...] = k_ref[...].astype(F32).T.astype(BF)
    vt[...] = v_ref[...].astype(F32).T.astype(BF)
    dk[...] = jnp.zeros_like(dk)
    dv[...] = jnp.zeros_like(dv)

    row = lax.broadcasted_iota(jnp.int32, (QM, 512), 0)
    col = lax.broadcasted_iota(jnp.int32, (QM, 512), 1)
    late = jnp.where(z * NY + (row >> 6) > spot, 2, 0)
    pick = jnp.where(col == (row & 31) * 16 + (row >> 5) + late, 1.0, 0.0).astype(BF)
    g_ref[...] = dot(pick, gz_ref[...].reshape(512, 512)).astype(BF)
    row = lax.broadcasted_iota(jnp.int32, (16, 512), 0)
    col = lax.broadcasted_iota(jnp.int32, (16, 512), 1)
    group = 2 * spot + 2 + (row & 1)
    band = jnp.minimum(group >> 3, NZ - 1)
    pick = jnp.where(
        (col == (row >> 1) * 128 + band * 16 + group - 8 * band) & (row < 8), 1.0, 0.0
    ).astype(BF)
    extra = dot(pick, gy_ref[...].reshape(512, 512)).astype(BF)
    for h in range(4):
        go_ref[8 * h : 8 * h + 8, :] = extra[0:8, HEAD * h : HEAD * (h + 1)]
        for j in range(NY):
            qo_ref[8 * h + 2 * j : 8 * h + 2 * j + 2, :] = heads_ref[h, j, MAIN : MAIN + 2, :]

    def span(c):
        return pl.ds(pl.multiple_of(c * CHUNK, 32), CHUNK)

    def block(q, g, qidx, width):
        qt = q.astype(F32).T.astype(BF)
        gt32 = g.astype(F32).T
        gt = gt32.astype(BF)

        peak = jnp.full((1, width), -jnp.inf, F32)
        for c in range(chunks):
            at = span(c)
            s = dot(k_ref[at, :], qt) * FACTOR
            s = jnp.where(kidx_ref[at, :] <= qidx, s, -jnp.inf)
            scores[at, :width] = s
            peak = jnp.maximum(peak, jnp.max(s, axis=0, keepdims=True))
        total = jnp.zeros((1, width), F32)
        for c in range(chunks):
            at = span(c)
            p = jnp.exp(scores[at, :width] - peak)
            scores[at, :width] = p
            total = total + jnp.sum(p, axis=0, keepdims=True)
        inverse = 1.0 / total
        out_t = jnp.zeros((HEAD, width), F32)
        for c in range(chunks):
            at = span(c)
            a = scores[at, :width] * inverse
            scores[at, :width] = a
            low = a.astype(BF)
            out_t = out_t + dot(vt[:, c * CHUNK : (c + 1) * CHUNK], low)
            dv[at, :] += dot(low, g)
        delta = jnp.sum(gt32 * out_t, axis=0, keepdims=True)
        dq_t = jnp.zeros((HEAD, width), F32)
        for c in range(chunks):
            at = span(c)
            da = dot(v_ref[at, :], gt)
            ds = (scores[at, :width] * (da - delta)).astype(BF)
            dq_t = dq_t + dot(kt[:, c * CHUNK : (c + 1) * CHUNK], ds)
            dk[at, :] += dot(ds, q)
        return out_t, (dq_t * FACTOR).T.astype(BF)

    row = lax.broadcasted_iota(jnp.int32, (QM, QM), 0)
    col = lax.broadcasted_iota(jnp.int32, (QM, QM), 1)
    turn = jnp.where(col == (row & 7) * 32 + (row >> 3), 1.0, 0.0).astype(BF)

    @pl.loop(0, 4)
    def _(h):
        q = heads_ref[h, :, 0:MAIN, :].reshape(QM, HEAD)
        out_t, dq = block(q, g_ref[:, lanes(h)], qidx_ref[...], QM)
        moved = lax.dot_general(
            turn, out_t.astype(BF), (((1,), (1,)), ((), ())), preferred_element_type=F32
        )
        om_ref[:, :, lanes(h)] = moved.astype(BF).reshape(NS, 8, HEAD)
        dq_ref[h, :, 0:MAIN, :] = dq.reshape(NY, MAIN, HEAD)

    out_t, dq = block(qo_ref[...], go_ref[...], qoidx_ref[...], QO)
    out = out_t.T.astype(BF)
    oo_ref[...] = jnp.zeros_like(oo_ref)
    dq_ref[:, :, MAIN:ROWS, :] = jnp.zeros((4, NY, ROWS - MAIN, HEAD), BF)
    for h in range(4):
        for j in range(NY):
            at = 8 * h + 2 * j
            oo_ref[j, 0:2, HEAD * h : HEAD * (h + 1)] = out[at : at + 2]
            dq_ref[h, j, MAIN : MAIN + 2, :] = dq[at : at + 2]
    for i, (ref, scale) in enumerate(((dk, FACTOR), (dv, 1.0))):
        for k in range(NZ):
            block_rows = (ref[k * QM : (k + 1) * QM, :] * scale).astype(BF)
            dkv_ref[i, k, :, 0:MAIN, :] = block_rows.reshape(NY, MAIN, HEAD)
        extra = (ref[KM:PATCHES, :] * scale).astype(BF)
        dkv_ref[i, :, :, MAIN:ROWS, :] = jnp.zeros((NZ, NY, ROWS - MAIN, HEAD), BF)
        for k in range(NZ):
            for j in range(NY):
                at = 2 * (k * NY + j)
                dkv_ref[i, k, j, MAIN : MAIN + 2, :] = extra[at : at + 2]


def attention(heads, kv, gy, gz, spot, kidx, qidx, qoidx):
    return pl.pallas_call(
        attention_kernel,
        in_specs=[VM] * 8,
        out_specs=[VM] * 4,
        out_shape=[
            jax.ShapeDtypeStruct((NS, 8, 512), BF),
            jax.ShapeDtypeStruct((NY, 8, 512), BF),
            jax.ShapeDtypeStruct((4, NY, ROWS, HEAD), BF),
            jax.ShapeDtypeStruct((2, NZ, NY, ROWS, HEAD), BF),
        ],
        scratch_shapes=[
            pltpu.VMEM((PATCHES, HEAD), BF),
            pltpu.VMEM((PATCHES, HEAD), BF),
            pltpu.VMEM((HEAD, PATCHES), BF),
            pltpu.VMEM((HEAD, PATCHES), BF),
            pltpu.VMEM((QM, 512), BF),
            pltpu.VMEM((QO, HEAD), BF),
            pltpu.VMEM((QO, HEAD), BF),
            pltpu.VMEM((PATCHES, QM), F32),
            pltpu.VMEM((PATCHES, HEAD), F32),
            pltpu.VMEM((PATCHES, HEAD), F32),
        ],
        compiler_params=pltpu.CompilerParams(vmem_limit_bytes=VMEM_LIMIT),
        name="attention",
    )(heads, kv, gy, gz, spot, kidx, qidx, qoidx)


def add(*parts):
    total = parts[0].astype(F32)
    for part in parts[1:]:
        total = total + part.astype(F32)
    return total.astype(BF)


def columns_kernel(
    dq, dkv, cols, ubuf, usum, dbuf, dsum, red, hs, hr, rs, rr, ls, lr
):
    z, y, x, c = here()
    n = x * 2 + c
    up, down = lax.rem(z + 1, NZ), lax.rem(z + NZ - 1, NZ)
    peers = []
    for j in range(1, NDP * NY):
        p, q = lax.rem(n + j // NY, NDP), lax.rem(y + j, NY)
        peers.append({"y": q, "x": p // 2, "c": lax.rem(p, 2)})
    greet(peers + [{"z": up}, {"z": down}])

    def plan(slot, j):
        k = lax.rem(y + j, NY)
        head = y * 4 + slot if slot < 4 else slot * 4 + y
        d, i = head // 3, lax.rem(head, 3)
        src = dq.at[slot, k] if slot < 4 else red.at[slot - 4, k]
        dst = cols.at[n, :, lanes(i)]
        there = lambda: send(
            src, dst, (hs.at[slot, j], hr.at[n, i]), y=k, x=d // 2, c=lax.rem(d, 2)
        )
        stay = lambda: pltpu.make_async_copy(src, dst, hr.at[n, i])
        return there, stay, d == n

    def start(slot):
        for j in range(1, NY):
            plan(slot, j)[0]().start()
        there, stay, own = plan(slot, 0)

        @pl.when(own)
        def _():
            stay().start()

        @pl.when(jnp.logical_not(own))
        def _():
            there().start()

    def sent(slot):
        for j in range(1, NY):
            plan(slot, j)[0]().wait_send()
        there, _, own = plan(slot, 0)

        @pl.when(jnp.logical_not(own))
        def _():
            there().wait_send()

    def at(k):
        return lax.rem(z + k, NZ)

    ups, downs = {}, {}
    for t in range(1, 5):
        for i in range(2):
            if t == 1:
                above, below = dkv.at[i, at(4)], dkv.at[i, at(5)]
            else:
                ups[t - 1, i].wait_recv()
                usum[i, t - 2] = add(ubuf[i, t - 2], dkv[i, at(5 - t)])
                above = usum.at[i, t - 2]
                if t < 4:
                    downs[t - 1, i].wait_recv()
                    dsum[i, t - 2] = add(dbuf[i, t - 2], dkv[i, at(4 + t)])
                    below = dsum.at[i, t - 2]
            ups[t, i] = send(above, ubuf.at[i, t - 1], (rs.at[t - 1, i], rr.at[t - 1, i]), z=up)
            ups[t, i].start()
            if t < 4:
                downs[t, i] = send(
                    below, dbuf.at[i, t - 1], (ls.at[t - 1, i], lr.at[t - 1, i]), z=down
                )
                downs[t, i].start()
        if t == 1:
            for slot in range(4):
                start(slot)
    for i in range(2):
        downs[3, i].wait_recv()
        ups[4, i].wait_recv()
        red[i] = add(ubuf[i, 3], dbuf[i, 2], dkv[i, z])
        start(4 + i)
    for p in range(NDP):
        for i in range(3):
            block = cols.at[p, :, i * HEAD : (i + 1) * HEAD]
            pltpu.make_async_copy(block, block, hr.at[p, i]).wait()
    for copy in (*ups.values(), *downs.values()):
        copy.wait_send()
    for slot in range(6):
        sent(slot)


def to_columns(dq, dkv):
    dma = pltpu.SemaphoreType.DMA
    part = (NY, ROWS, HEAD)
    return pl.pallas_call(
        columns_kernel,
        in_specs=[VM, VM],
        out_specs=ANY,
        out_shape=jax.ShapeDtypeStruct((NDP, ROWS, COLS), BF),
        scratch_shapes=[
            pltpu.VMEM((2, 4, *part), BF),
            pltpu.VMEM((2, 3, *part), BF),
            pltpu.VMEM((2, 3, *part), BF),
            pltpu.VMEM((2, 2, *part), BF),
            pltpu.VMEM((2, *part), BF),
            dma((6, NY)),
            dma((NDP, 3)),
            dma((4, 2)),
            dma((4, 2)),
            dma((3, 2)),
            dma((3, 2)),
        ],
        compiler_params=pltpu.CompilerParams(
            collective_id=2, has_side_effects=True, vmem_limit_bytes=VMEM_LIMIT
        ),
        name="to_columns",
    )(dq, dkv)


def products_kernel(main_ref, over_ref, cols_ref, weight_ref, part_ref, back_ref, cm, co, over_rows):
    @pl.when(pl.program_id(0) == 0)
    def _():
        for n in range(NDP):
            cm[MAIN * n : MAIN * (n + 1), :] = cols_ref[n, 0:MAIN, :]
            co[2 * n : 2 * n + 2, :] = cols_ref[n, MAIN : MAIN + 2, :]

    width = weight_ref.shape[0]
    for n in range(NDP):
        over_rows[2 * n : 2 * n + 2, :] = over_ref[n]
    part = dot_t(main_ref[...].reshape(NDP * MAIN, width), cm[...]) + dot_t(over_rows[...], co[...])
    part_ref[0] = part.astype(BF).reshape(NY, HEAD, COLS)
    turn = (((1,), (1,)), ((), ()))
    back = lax.dot_general(cm[...], weight_ref[...], turn, preferred_element_type=F32)
    extra = lax.dot_general(co[...], weight_ref[...], turn, preferred_element_type=F32)
    back = back.astype(BF)
    extra = extra.astype(BF)
    for n in range(NDP):
        back_ref[n, 0:MAIN, :] = back[MAIN * n : MAIN * (n + 1)]
        back_ref[n, MAIN:ROWS, :] = jnp.zeros((ROWS - MAIN, width), BF)
        back_ref[n, MAIN : MAIN + 2, :] = extra[2 * n : 2 * n + 2]


def products(all_main, all_over, cols, weight):
    steps = NZ
    width = DG // steps
    return pl.pallas_call(
        products_kernel,
        grid=(steps,),
        in_specs=[
            pl.BlockSpec((NDP, MAIN, width), lambda i: (0, 0, i)),
            pl.BlockSpec((NDP, 2, width), lambda i: (0, 0, i)),
            pl.BlockSpec((NDP, ROWS, COLS), lambda i: (0, 0, 0)),
            pl.BlockSpec((width, COLS), lambda i: (i, 0)),
        ],
        out_specs=[
            pl.BlockSpec((1, NY, HEAD, COLS), lambda i: (i, 0, 0, 0)),
            pl.BlockSpec((NDP, ROWS, width), lambda i: (0, 0, i)),
        ],
        out_shape=[
            jax.ShapeDtypeStruct((NZ, NY, HEAD, COLS), BF),
            jax.ShapeDtypeStruct((NDP, ROWS, DG), BF),
        ],
        scratch_shapes=[
            pltpu.VMEM((NDP * MAIN, COLS), BF),
            pltpu.VMEM((16, COLS), BF),
            pltpu.VMEM((16, width), BF),
        ],
        compiler_params=pltpu.CompilerParams(vmem_limit_bytes=VMEM_LIMIT),
        name="products",
    )(all_main, all_over, cols, weight)


def sums_kernel(
    back, w, om, oo,
    pooled, over_all, wgrad, am, ao,
    own, sib, chip, xa, xb, xr, xl, sxa, sxb,
    ya, yb, yr, yl, sa, sb, wy, ubuf, usum, dbuf, dsum, omz, ov, oz,
    local, cs, cr, xs, xrv, ws, wr, us, ur, ds, dr, zs, zr, os_, or_,
):
    z, y, x, c = here()
    right, left, far = lax.rem(x + 1, NX), lax.rem(x + 3, NX), lax.rem(x + 2, NX)
    yn, yp, yf = lax.rem(y + 1, NY), lax.rem(y + 3, NY), lax.rem(y + 2, NY)
    up, down = lax.rem(z + 1, NZ), lax.rem(z + NZ - 1, NZ)
    ys_at = [lax.rem(y + j, NY) for j in range(NY)]
    zs_at = [lax.rem(z + j, NZ) for j in range(NZ)]
    greet(
        [{"y": ys_at[j]} for j in range(1, NY)]
        + [{"z": zs_at[j]} for j in range(1, NZ)]
        + [{"x": right}, {"x": left}, {"c": 1 - c}]
    )
    copies = []

    def go(src, dst, pair, **device):
        copy = send(src, dst, pair, **device)
        copy.start()
        copies.append(copy)
        return copy

    order = (far, right, left, x)
    halves = [
        go(back.at[p * 2 + 1 - c], sib.at[p], (cs.at[k], cr.at[k]), c=1 - c)
        for k, p in enumerate(order)
    ]
    loads = [
        pltpu.make_async_copy(back.at[p * 2 + c], own.at[p], local.at[k])
        for k, p in enumerate(order)
    ]
    for copy in loads:
        copy.start()

    lo, hi = pl.ds(0, 4), pl.ds(4, 4)
    w_a = go(w.at[lo, yf], ya, (ws.at[0], wr.at[0]), y=yn)
    w_b = go(w.at[hi, yf], yb, (ws.at[1], wr.at[1]), y=yp)
    w_hi = go(w.at[hi, yn], yr.at[hi], (ws.at[2], wr.at[2]), y=yn)
    w_lo = go(w.at[lo, yp], yl.at[lo], (ws.at[3], wr.at[3]), y=yp)

    rows_z = [
        go(om.at[zs_at[j]], omz.at[z], (zs.at[0, j], zr.at[0, j]), z=zs_at[j])
        for j in range(1, NZ)
    ]
    stay_z = pltpu.make_async_copy(om.at[z], omz.at[z], local.at[4])
    stay_z.start()

    first, second = pl.ds(0, DG // 2), pl.ds(DG // 2, DG // 2)
    for k, p in enumerate(order):
        loads[k].wait()
        halves[k].wait_recv()
        chip[p] = add(own[p], sib[p])
        if k == 0:
            x_a = go(chip.at[p, :, first], xa, (xs.at[0], xrv.at[0]), x=right)
            x_b = go(chip.at[p, :, second], xb, (xs.at[1], xrv.at[1]), x=left)
        if k == 1:
            x_hi = go(chip.at[p, :, second], xr.at[:, second], (xs.at[2], xrv.at[2]), x=right)
        if k == 2:
            x_lo = go(chip.at[p, :, first], xl.at[:, first], (xs.at[3], xrv.at[3]), x=left)

    w_a.wait_recv()
    sa[...] = add(ya[...], w[lo, yn])
    w_lo2 = go(sa, yr.at[lo], (ws.at[4], wr.at[4]), y=yn)
    w_b.wait_recv()
    sb[...] = add(yb[...], w[hi, yp])
    w_hi2 = go(sb, yl.at[hi], (ws.at[5], wr.at[5]), y=yp)
    x_a.wait_recv()
    sxa[...] = add(xa[...], chip[right, :, first])
    x_lo2 = go(sxa, xr.at[:, first], (xs.at[4], xrv.at[4]), x=right)
    x_b.wait_recv()
    sxb[...] = add(xb[...], chip[left, :, second])
    x_hi2 = go(sxb, xl.at[:, second], (xs.at[5], xrv.at[5]), x=left)

    for copy in rows_z:
        copy.wait_recv()
    stay_z.wait()
    rows_y = []
    for j in range(1, NY):
        k = ys_at[j]
        rows_y.append(go(omz.at[:, k], am.at[y], (os_.at[0, j], or_.at[0, j]), y=k))
        rows_y.append(go(oo.at[k], ao.at[y], (os_.at[1, j], or_.at[1, j]), y=k))
    stay_y = [
        pltpu.make_async_copy(omz.at[:, y], am.at[y], local.at[5]),
        pltpu.make_async_copy(oo.at[y], ao.at[y], local.at[6]),
    ]
    for copy in stay_y:
        copy.start()

    for copy in (x_hi, x_lo, x_lo2, x_hi2):
        copy.wait_recv()
    pooled[...] = add(chip[x], xr[...], xl[...])
    ov[...] = pooled[MAIN : MAIN + 2, :]
    over_z = [
        go(ov, oz.at[z], (zs.at[1, j], zr.at[1, j]), z=zs_at[j]) for j in range(1, NZ)
    ]
    keep_z = pltpu.make_async_copy(ov, oz.at[z], local.at[7])
    keep_z.start()

    for copy in (w_hi, w_lo, w_lo2, w_hi2):
        copy.wait_recv()
    wy[...] = add(w[:, y], yr[...], yl[...])

    def at(k):
        return lax.rem(z + k, NZ)

    ups, downs = {}, {}
    over_y = []
    for t in range(1, 5):
        if t == 1:
            above, below = wy.at[at(4)], wy.at[at(5)]
        else:
            ups[t - 1].wait_recv()
            usum[t - 2] = add(ubuf[t - 2], wy[at(5 - t)])
            above = usum.at[t - 2]
            if t < 4:
                downs[t - 1].wait_recv()
                dsum[t - 2] = add(dbuf[t - 2], wy[at(4 + t)])
                below = dsum.at[t - 2]
        ups[t] = go(above, ubuf.at[t - 1], (us.at[t - 1], ur.at[t - 1]), z=up)
        if t < 4:
            downs[t] = go(below, dbuf.at[t - 1], (ds.at[t - 1], dr.at[t - 1]), z=down)
        if t == 1:
            for copy in over_z:
                copy.wait_recv()
            keep_z.wait()
            for j in range(1, NY):
                over_y.append(
                    go(oz, over_all.at[y], (os_.at[2, j], or_.at[2, j]), y=ys_at[j])
                )
            keep_y = pltpu.make_async_copy(oz, over_all.at[y], local.at[8])
            keep_y.start()
    downs[3].wait_recv()
    ups[4].wait_recv()
    wgrad[...] = ubuf[3].astype(F32) + dbuf[2].astype(F32) + wy[z].astype(F32)
    for copy in (*over_y, *rows_y):
        copy.wait_recv()
    for copy in copies:
        copy.wait_send()
    for copy in (*stay_y, keep_y):
        copy.wait()


def sums(back, part, om, oo):
    dma = pltpu.SemaphoreType.DMA
    rows = (ROWS, DG)
    half = (ROWS, DG // 2)
    block = (HEAD, COLS)
    return pl.pallas_call(
        sums_kernel,
        in_specs=[ANY, VM, ANY, ANY],
        out_specs=[VM, ANY, VM, ANY, ANY],
        out_shape=[
            jax.ShapeDtypeStruct(rows, BF),
            jax.ShapeDtypeStruct((NY, NZ, 2, DG), BF),
            jax.ShapeDtypeStruct(block, F32),
            jax.ShapeDtypeStruct((NY, NZ, 8, 512), BF),
            jax.ShapeDtypeStruct((NY, 8, 512), BF),
        ],
        scratch_shapes=[
            *[pltpu.VMEM((NX, *rows), BF)] * 3,
            *[pltpu.VMEM(half, BF)] * 2,
            *[pltpu.VMEM(rows, BF)] * 2,
            *[pltpu.VMEM(half, BF)] * 2,
            *[pltpu.VMEM((4, *block), BF)] * 2,
            *[pltpu.VMEM((8, *block), BF)] * 2,
            *[pltpu.VMEM((4, *block), BF)] * 2,
            pltpu.VMEM((8, *block), BF),
            pltpu.VMEM((4, *block), BF),
            pltpu.VMEM((3, *block), BF),
            pltpu.VMEM((3, *block), BF),
            pltpu.VMEM((2, *block), BF),
            pltpu.VMEM((NZ, NY, 8, 512), BF),
            pltpu.VMEM((2, DG), BF),
            pltpu.VMEM((NZ, 2, DG), BF),
            dma((9,)),
            dma((4,)),
            dma((4,)),
            dma((6,)),
            dma((6,)),
            dma((6,)),
            dma((6,)),
            dma((4,)),
            dma((4,)),
            dma((3,)),
            dma((3,)),
            dma((2, NZ)),
            dma((2, NZ)),
            dma((3, NY)),
            dma((3, NY)),
        ],
        compiler_params=pltpu.CompilerParams(
            collective_id=3, has_side_effects=True, vmem_limit_bytes=VMEM_LIMIT
        ),
        name="sums",
    )(back, part, om, oo)


def body(byte_states, byte_patch, patch_owner, qkv_weight, attention_output_gradient):
    z, y = lax.axis_index("z"), lax.axis_index("y")
    s = z * NY + y
    main, over, slot, flag, band = pool(
        byte_patch, patch_owner, byte_states, attention_output_gradient
    )
    all_main, all_over, found, grad_y, grad_z = gather_rows(main, over, flag, band)
    spot = found[0, 0].astype(jnp.int32)

    owners = patch_owner[0].reshape(66, 32)
    who = jnp.arange(32, dtype=jnp.int32)
    place = jnp.sum(
        jnp.where(owners[:, :, None] == who[None, None, :], who[None, :, None], 0), axis=1
    )
    index = place + 32 * jnp.arange(66, dtype=jnp.int32)[:, None]
    flat = index.reshape(-1)
    row = jnp.arange(2048, dtype=jnp.int32)
    main_index = jnp.where(row < MAIN * (spot + 1), flat[:2048], flat[64:])
    over_index = lax.dynamic_slice_in_dim(index, 2 * spot + 2, 2, 0).T.reshape(-1)
    key_index = jnp.concatenate([main_index, over_index])
    query_index = lax.dynamic_slice_in_dim(main_index, z * QM, QM)
    query_over_index = lax.dynamic_slice_in_dim(over_index, z * 8, 8)

    proj = project(all_main, all_over, qkv_weight)
    heads, kv = to_heads(proj)
    om, oo, dq, dkv = attention(
        heads, kv, grad_y, grad_z, found,
        key_index[:, None], query_index[None], jnp.tile(query_over_index, 4)[None],
    )

    cols = to_columns(dq, dkv)
    part, back = products(all_main, all_over, cols, qkv_weight)
    pooled, over_back, weight_grad, am, ao = sums(back, part, om.reshape(NZ, NY, 8, 512), oo)
    state_grad, att = spread(slot, pooled, over_back, am, ao, found)
    return att, state_grad, weight_grad


def solution(mesh):
    finer = Mesh(mesh.devices.reshape(NZ, NY, NX, NC), ("z", "y", "x", "c"))
    placed = (P(DP, SEQ, None), P(DP, SEQ), P(DP, None), P(None, DP), P(DP, SEQ, None))
    return jax.shard_map(
        body,
        mesh=finer,
        in_specs=placed,
        out_specs=(P(DP, SEQ, None), P(DP, SEQ, None), P(SEQ, DP)),
        check_vma=False,
    )
```

time: 503 us -> 214 us (0.43)
  Pallas kernels: 0 us -> 204 us
  waiting for transfers between devices: 154 us -> 0 us
  blocking collectives: 153 us -> 0 us
  local copies, waits for them, and re-layouts: 68.2 us -> 6.21 us
  matrix products: 57.3 us -> 0 us
  starting transfers between devices: 26.4 us -> 0 us
  other arithmetic: 21.8 us -> 0.83 us
  between operations: 18 us -> 1.37 us
    pallas_call x0 -> x9, Pallas kernels: none -> 204 us  [the longest x1 52.7 us: sums(): pl.pallas_call(sums_kernel, in_specs=[ANY, VM, ANY, ANY], out_specs=[VM,...]
    all_to_all x3 -> x0, blocking collectives: 86 us -> none  [the longest x1 60.6 us: sum_at_owner(): lax.all_to_all(blocks, axis, split_axis=0, concat_axis=0, tiled=True)]
    all_to_all x3 -> x0, waiting for transfers between devices: 55.1 us -> none  [the longest x1 26 us: body(): lax.all_to_all(send_rows.reshape(seq_count, capacity, -1), SEQ, split_axi...]
    reduce_scatter x3 -> x0, waiting for transfers between devices: 54.6 us -> none  [the longest x1 54.5 us: sum_by_axis(): shard = lax.psum_scatter(shard, axis, scatter_dimension=dim, tiled=True)]
    unnamed x3 -> x0, blocking collectives: 53.5 us -> none
    dot_general x12 -> x0, matrix products: 48.5 us -> none  [the longest x2 9.6 us: contract_rows(): lax.dot_general(left, right, (((0,), (0,)), ((), ())), preferred_element_...]
    all_gather x2 -> x0, waiting for transfers between devices: 43.6 us -> none  [the longest x1 32.1 us: body(): all_rows = lax.all_gather(own_rows, 'dp', axis=0, tiled=True)]
    all_to_all x3 -> x0, starting transfers between devices: 22.4 us -> none  [the longest x1 11.5 us: body(): lax.all_to_all(send_index.reshape(seq_count, capacity), SEQ, split_axis=0...]
  transfers between devices with their start and end apart: 9 -> 0, of which waited for: 6 -> 0; matrix products, arithmetic and copies ran while one was open for 9% -> 0% of each run, Pallas kernels for 0% -> 0%
where the time goes in v1:
time: 214 us; the launch traced here: 213 us
  Pallas kernels  204 us (95%)
  local copies, waits for them, and re-layouts  6.21 us (3%)
    pallas_call x1, Pallas kernels, sums(): pl.pallas_call(sums_kernel, in_specs=[ANY, VM, ANY, ANY], out_specs=[VM,...  52.7 us
    pallas_call x1, Pallas kernels, gather_rows(): pl.pallas_call(gather_kernel, in_specs=[ANY, ANY, VM, ANY], out_specs=[AN...  44.4 us
    pallas_call x1, Pallas kernels, to_columns(): pl.pallas_call(columns_kernel, in_specs=[VM, VM], out_specs=ANY, out_shap...  32.6 us
    pallas_call x1, Pallas kernels, to_heads(): pl.pallas_call(heads_kernel, in_specs=[ANY], out_specs=[ANY, ANY], out_sh...  29.2 us
    pallas_call x1, Pallas kernels, attention(): pl.pallas_call(attention_kernel, in_specs=[VM] * 8, out_specs=[VM] * 4, o...  19.2 us
    pallas_call x1, Pallas kernels, products(): pl.pallas_call(products_kernel, grid=(steps,), in_specs=[pl.BlockSpec((ND...  11.1 us
    pallas_call x1, Pallas kernels, project(): pl.pallas_call(project_kernel, grid=(steps,), in_specs=[pl.BlockSpec((NDP...  6.3 us
    pallas_call x1, Pallas kernels, spread(): pl.pallas_call(spread_kernel, grid=(steps,), in_specs=[pl.BlockSpec((1, B...  4.51 us

profile of v1, /device:TPU:6, one launch (start us, length us, event | category | flops | bytes accessed | tf_op | source)
XLA Modules:
  0.0 212.8 jit_solution(5932338468941643492)
XLA Ops:
  0.6 0.7 reduce
  1.4 0.1 eq.15
  1.4 0.1 copy.11
  1.5 0.1 select_reduce_fusion
  1.7 0.1 copy.13
  1.9 0.1 copy.12
  1.9 0.1 slice.17
  2.0 4.4 %pool.1 = (bf16[64,4096]{1,0:T(8,128)(2,1)}, bf16[4,16,4096]{2,1,0:T(8,128)(2,1)}, s32[1,256]{1,0:T(1,128)}, f32[8,128]{1,0:T(8,128)}, bf16[8,16,2048]{2,1,0:T(8,128)(2,1)}) custom-call(s32[1,256]{1,0:T(1,128)} %ids_ref.1, s32[1,2112]{1,0:T(1,128)} %owner_ref.1, bf16[1,256,4096]{2,1,0:T(8,128)(2,1)} %states_ref.1, bf16[1,66,2048]{2,1,0:T(8,128)(2,1)} %grad_ref.1), custom_call_target="tpu_custom_call" | custom-call | tf_op jit(solution)/shard_map/pool/pallas_call | solution.py:77
  6.4 44.4 %gather_rows.1 = (bf16[8,64,4096]{2,1,0:T(8,128)(2,1)}, bf16[8,2,4096]{2,1,0:T(2,128)(2,1)}, f32[8,128]{1,0:T(8,128)}, bf16[4,8,16,512]{3,2,1,0:T(8,128)(2,1)}, bf16[8,4,16,512]{3,2,1,0:T(8,128)(2,1)}) custom-call(bf16[64,4096]{1,0:T(8,128)(2,1)} %get-tuple-element.29.main, bf16[4,16,4096]{2,1,0:T(8,128)(2,1)} %get-tuple-element.30.over, ...), custom_call_target="tpu_custom_call" | custom-call | tf_op jit(solution)/shard_map/gather_rows/pallas_call | solution.py:267
  50.8 1.2 slice.15
  52.7 0.1 dynamic-slice_bitcast_fusion
  52.7 0.1 reshape.33
  52.8 0.1 dynamic_slice.11
  52.9 0.6 dynamic_slice.10
  53.6 0.6 broadcast_in_dim_tile.3.qoidx_ref
  54.2 6.3 %project.1.proj = bf16[8,72,384]{2,1,0:T(8,128)(2,1)} custom-call(bf16[8,64,4096]{2,1,0:T(8,128)(2,1)} %get-tuple-element.33.main_ref, bf16[8,2,4096]{2,1,0:T(2,128)(2,1)} %get-tuple-element.34.over_ref, bf16[4096,384]{1,0:T(8,128)(2,1)} %weight_ref.3), custom_call_target="tpu_custom_call" | custom-call | tf_op jit(solution)/shard_map/project/pallas_call | solution.py:388
  60.5 1.4 broadcast_in_dim.25.kidx_ref
  61.8 29.2 %to_heads.1 = (bf16[6,4,72,128]{3,2,1,0:T(8,128)(2,1)}, bf16[2,8,4,72,128]{4,3,2,1,0:T(8,128)(2,1)}) custom-call(bf16[8,72,384]{2,1,0:T(8,128)(2,1)} %project.1.proj), custom_call_target="tpu_custom_call" | custom-call | tf_op jit(solution)/shard_map/to_heads/pallas_call | solution.py:497
  91.0 19.2 %attention.1 = (bf16[32,8,512]{2,1,0:T(8,128)(2,1)}, bf16[4,8,512]{2,1,0:T(8,128)(2,1)}, bf16[4,4,72,128]{3,2,1,0:T(8,128)(2,1)}, bf16[2,8,4,72,128]{4,3,2,1,0:T(8,128)(2,1)}) custom-call(bf16[6,4,72,128]{3,2,1,0:T(8,128)(2,1)} %get-tuple-element.35.heads_ref, bf16[2,8,4,72,128]{4,3,2,1,0:T(8,128)(2,1)} %get-tuple-element.36.kv_ref, ...), custom_call_target="tpu_custom_call" | custom-call | tf_op jit(solution)/shard_map/attention/pallas_call | solution.py:639
  110.2 32.6 %to_columns.1.cols_ref = bf16[8,72,384]{2,1,0:T(8,128)(2,1)} custom-call(bf16[4,4,72,128]{3,2,1,0:T(8,128)(2,1)} %get-tuple-element.40.dq, bf16[2,8,4,72,128]{4,3,2,1,0:T(8,128)(2,1)} %get-tuple-element.41.dkv), custom_call_target="tpu_custom_call" | custom-call | tf_op jit(solution)/shard_map/to_columns/pallas_call | solution.py:763
  142.8 11.1 %products.1 = (bf16[8,4,128,384]{3,2,1,0:T(8,128)(2,1)}, bf16[8,72,4096]{2,1,0:T(8,128)(2,1)}) custom-call(bf16[8,64,4096]{2,1,0:T(8,128)(2,1)} %get-tuple-element.33.main_ref, bf16[8,2,4096]{2,1,0:T(2,128)(2,1)} %get-tuple-element.34.over_ref, bf16[8,72,384]{2,1,0:T(8,128)(2,1)} %to_columns.1.cols_ref, bf16[4096,384]{1,0:T(8,128)(2,1)} %weight_ref.3), custom_call_target="tpu_custom_call" | custom-call | tf_op jit(solution)/shard_map/products/pallas_call | solution.py:814
  153.9 52.7 %sums.1 = (bf16[72,4096]{1,0:T(8,128)(2,1)}, bf16[4,8,2,4096]{3,2,1,0:T(2,128)(2,1)}, f32[128,384]{1,0:T(8,128)}, bf16[4,8,8,512]{3,2,1,0:T(8,128)(2,1)}, bf16[4,8,512]{2,1,0:T(8,128)(2,1)}) custom-call(bf16[8,72,4096]{2,1,0:T(8,128)(2,1)} %get-tuple-element.42.back, bf16[8,4,128,384]{3,2,1,0:T(8,128)(2,1)} %get-tuple-element.43.w, ...), custom_call_target="tpu_custom_call" | custom-call | tf_op jit(solution)/shard_map/sums/pallas_call | solution.py:992
  206.7 4.5 %spread.1 = (bf16[1,256,4096]{2,1,0:T(8,128)(2,1)}, bf16[1,66,2048]{2,1,0:T(8,128)(2,1)}) custom-call(s32[1,256]{1,0:T(1,128)} %get-tuple-element.28.slot_ref, bf16[72,4096]{1,0:T(8,128)(2,1)} %get-tuple-element.46.pooled_ref, bf16[4,8,2,4096]{3,2,1,0:T(2,128)(2,1)} %get-tuple-element.47.over_ref, bf16[4,8,8,512]{3,2,1,0:T(8,128)(2,1)} %get-tuple-element.48.am_ref, ...), custom_call_target="tpu_custom_call" | custom-call | tf_op jit(solution)/shard_map/spread/pallas_call | solution.py:333
  211.2 1.6 copy.16
  (7 shorter events, 0.2 us)

commit v2 on v1

--- a/solution.py
+++ b/solution.py
@@ -107,6 +107,13 @@
 VM = pl.BlockSpec(memory_space=pltpu.VMEM)
 
 
+def add(*parts):
+    total = parts[0].astype(F32)
+    for part in parts[1:]:
+        total = total + part.astype(F32)
+    return total.astype(BF)
+
+
 def here():
     return [lax.axis_index(name) for name in ("z", "y", "x", "c")]
 
@@ -126,9 +133,9 @@
 
 
 def gather_kernel(
-    main, over, flag, band,
+    main, over, flag, band, grad,
     all_main, all_over, spot, gy, gz,
-    ybuf, zsrc, zbuf, mine, fy, fsum, fz,
+    ybuf, zsrc, zbuf, mine, fy, fsum, fz, gband,
     local, main_s, main_r, ys, yr, zs, zr, os_, or_,
 ):
     z, y, x, c = here()
@@ -136,12 +143,25 @@
     ys_at = [lax.rem(y + j, NY) for j in range(NY)]
     zs_at = [lax.rem(z + j, NZ) for j in range(NZ)]
     dp_at = [lax.rem(n + j, NDP) for j in range(NDP)]
-    right, left, other = lax.rem(x + 1, NX), lax.rem(x + 3, NX), 1 - c
+    right, left, twin = lax.rem(x + 1, NX), lax.rem(x + 3, NX), 1 - c
     greet(
         [{"y": ys_at[j]} for j in range(1, NY)]
         + [{"z": zs_at[j]} for j in range(1, NZ)]
         + [{"x": p // 2, "c": lax.rem(p, 2)} for p in dp_at[1:]]
     )
+    copies, stays = [], []
+
+    def go(src, dst, pair, **device):
+        copy = send(src, dst, pair, **device)
+        copy.start()
+        copies.append(copy)
+        return copy
+
+    def stay(src, dst):
+        copy = pltpu.make_async_copy(src, dst, local.at[len(stays)])
+        copy.start()
+        stays.append(copy)
+        return copy
 
     def half(block, i):
         return block.at[pl.ds(32 * i, 32), :]
@@ -149,58 +169,48 @@
     def pair(i):
         return main_s.at[i], main_r.at[i]
 
-    mine_out = all_main.at[n]
-    first = [
-        send(main, mine_out, pair(1), x=right),
-        send(main, mine_out, pair(2), x=left),
-        send(main, mine_out, pair(0), c=other),
-    ]
-    for copy in first:
-        copy.start()
-    keep = [pltpu.make_async_copy(main, mine_out, local.at[0])]
+    def columns(h):
+        return pl.ds(pl.multiple_of(h * 512, 512), 512)
 
     stage_y = []
     for j in range(1, NY):
-        stage_y.append(send(over.at[ys_at[j]], ybuf.at[y], (ys.at[0, j], yr.at[0, j]), y=ys_at[j]))
-        stage_y.append(send(flag, fy.at[y], (ys.at[1, j], yr.at[1, j]), y=ys_at[j]))
-    here_y = [
-        pltpu.make_async_copy(over.at[y], ybuf.at[y], local.at[1]),
-        pltpu.make_async_copy(flag, fy.at[y], local.at[2]),
+        k = ys_at[j]
+        stage_y.append(go(over.at[k], ybuf.at[y], (ys.at[0, j], yr.at[0, j]), y=k))
+        stage_y.append(go(flag, fy.at[y], (ys.at[1, j], yr.at[1, j]), y=k))
+    here_y = [stay(over.at[y], ybuf.at[y]), stay(flag, fy.at[y])]
+
+    mine_out = all_main.at[n]
+    to_right = go(main, mine_out, pair(1), x=right)
+    to_left = go(main, mine_out, pair(2), x=left)
+    to_other = go(main, mine_out, pair(0), c=twin)
+    stay(main, mine_out)
+
+    bands_z = [
+        go(band.at[zs_at[j]], gband.at[z], (zs.at[2, j], zr.at[2, j]), z=zs_at[j])
+        for j in range(1, NZ)
     ]
-    for copy in stage_y + here_y + keep:
-        copy.start()
-
-    def columns(h):
-        return pl.ds(pl.multiple_of(h * 512, 512), 512)
-
-    grads_y = [
-        send(band.at[:, :, columns(ys_at[j])], gy.at[y], (ys.at[2, j], yr.at[2, j]), y=ys_at[j])
-        for j in range(1, NY)
-    ]
-    keep_y = pltpu.make_async_copy(band.at[:, :, columns(y)], gy.at[y], local.at[3])
-    for copy in grads_y + [keep_y]:
-        copy.start()
+    here_band = stay(band.at[z], gband.at[z])
 
     for copy in stage_y:
         copy.wait_recv()
     for copy in here_y:
         copy.wait()
-    rows = (
-        ybuf[0].astype(F32) + ybuf[1].astype(F32) + ybuf[2].astype(F32) + ybuf[3].astype(F32)
-    ).astype(BF)
+    rows = add(ybuf[0], ybuf[1], ybuf[2], ybuf[3])
     for k in range(NZ):
         zsrc[k] = rows[2 * k : 2 * k + 2]
     fsum[...] = fy[0] + fy[1] + fy[2] + fy[3]
     stage_z = []
     for j in range(1, NZ):
-        stage_z.append(send(zsrc.at[zs_at[j]], zbuf.at[z], (zs.at[0, j], zr.at[0, j]), z=zs_at[j]))
-        stage_z.append(send(fsum, fz.at[z], (zs.at[1, j], zr.at[1, j]), z=zs_at[j]))
-    here_z = [
-        pltpu.make_async_copy(zsrc.at[z], zbuf.at[z], local.at[4]),
-        pltpu.make_async_copy(fsum, fz.at[z], local.at[5]),
+        k = zs_at[j]
+        stage_z.append(go(zsrc.at[k], zbuf.at[z], (zs.at[0, j], zr.at[0, j]), z=k))
+        stage_z.append(go(fsum, fz.at[z], (zs.at[1, j], zr.at[1, j]), z=k))
+    here_z = [stay(zsrc.at[z], zbuf.at[z]), stay(fsum, fz.at[z])]
+    grads_y = [
+        go(grad.at[0, :, columns(ys_at[j])], gy.at[y], (ys.at[2, j], yr.at[2, j]), y=ys_at[j])
+        for j in range(1, NY)
     ]
-    for copy in stage_z + here_z:
-        copy.start()
+    stay(grad.at[0, :, columns(y)], gy.at[y])
+
     for copy in stage_z:
         copy.wait_recv()
     for copy in here_z:
@@ -213,66 +223,54 @@
     mine[...] = total.astype(BF)
     spot[...] = found
     overs = [
-        send(mine, all_over.at[n], (os_.at[j], or_.at[j]), x=dp_at[j] // 2, c=lax.rem(dp_at[j], 2))
+        go(mine, all_over.at[n], (os_.at[j], or_.at[j]), x=dp_at[j] // 2, c=lax.rem(dp_at[j], 2))
         for j in range(1, NDP)
     ]
-    keep_o = pltpu.make_async_copy(mine, all_over.at[n], local.at[6])
-    for copy in overs + [keep_o]:
-        copy.start()
-
-    for copy in grads_y:
-        copy.wait_recv()
-    keep_y.wait()
-    grads_z = [
-        send(gy.at[:, zs_at[j]], gz.at[z], (zs.at[2, j], zr.at[2, j]), z=zs_at[j])
-        for j in range(1, NZ)
-    ]
-    keep_z = pltpu.make_async_copy(gy.at[:, z], gz.at[z], local.at[7])
-    for copy in grads_z + [keep_z]:
-        copy.start()
+    stay(mine, all_over.at[n])
 
     from_left = all_main.at[left * 2 + c]
     from_right = all_main.at[right * 2 + c]
     far = all_main.at[lax.rem(x + 2, NX) * 2 + c]
-    first[0].wait_recv()
-    on_right = send(half(from_left, 0), half(from_left, 0), pair(3), x=right)
-    side_left = send(from_left, from_left, pair(5), c=other)
-    on_right.start()
-    first[1].wait_recv()
-    on_left = send(half(from_right, 1), half(from_right, 1), pair(4), x=left)
-    side_right = send(from_right, from_right, pair(6), c=other)
-    on_left.start()
-    side_left.start()
-    side_right.start()
+    to_right.wait_recv()
+    on_right = go(half(from_left, 0), half(from_left, 0), pair(3), x=right)
+    side_left = go(from_left, from_left, pair(5), c=twin)
+    to_left.wait_recv()
+    on_left = go(half(from_right, 1), half(from_right, 1), pair(4), x=left)
+    side_right = go(from_right, from_right, pair(6), c=twin)
+
+    for copy in bands_z:
+        copy.wait_recv()
+    here_band.wait()
+    bands_y = [
+        go(gband.at[:, :, columns(ys_at[j])], gz.at[:, y], (ys.at[3, j], yr.at[3, j]), y=ys_at[j])
+        for j in range(1, NY)
+    ]
+    stay(gband.at[:, :, columns(y)], gz.at[:, y])
+
     on_right.wait_recv()
-    side_a = send(half(far, 0), half(far, 0), pair(7), c=other)
-    side_a.start()
+    side_a = go(half(far, 0), half(far, 0), pair(7), c=twin)
     on_left.wait_recv()
-    side_b = send(half(far, 1), half(far, 1), pair(8), c=other)
-    side_b.start()
-    first[2].wait_recv()
-    for copy in (side_left, side_right, side_a, side_b, *overs, *grads_z):
+    side_b = go(half(far, 1), half(far, 1), pair(8), c=twin)
+    for copy in (to_other, side_left, side_right, side_a, side_b, *overs, *grads_y, *bands_y):
         copy.wait_recv()
-    for copy in (
-        *first, on_right, on_left, side_left, side_right, side_a, side_b,
-        *stage_y, *stage_z, *overs, *grads_y, *grads_z,
-    ):
+    for copy in copies:
         copy.wait_send()
-    for copy in (*keep, keep_o, keep_z):
-        copy.wait()
-
-
-def gather_rows(main, over, flag, band):
+    for copy in stays:
+        if not any(copy is other for other in (*here_y, *here_z, here_band)):
+            copy.wait()
+
+
+def gather_rows(main, over, flag, band, grad):
     dma = pltpu.SemaphoreType.DMA
     return pl.pallas_call(
         gather_kernel,
-        in_specs=[ANY, ANY, VM, ANY],
+        in_specs=[ANY, ANY, VM, ANY, ANY],
         out_specs=[ANY, ANY, VM, ANY, ANY],
         out_shape=[
             jax.ShapeDtypeStruct((NDP, MAIN, DG), BF),
             jax.ShapeDtypeStruct((NDP, 2, DG), BF),
             jax.ShapeDtypeStruct((8, 128), F32),
-            jax.ShapeDtypeStruct((NY, NZ, 16, 512), BF),
+            jax.ShapeDtypeStruct((NY, 66, 512), BF),
             jax.ShapeDtypeStruct((NZ, NY, 16, 512), BF),
         ],
         scratch_shapes=[
@@ -283,11 +281,12 @@
             pltpu.VMEM((NY, 8, 128), F32),
             pltpu.VMEM((8, 128), F32),
             pltpu.VMEM((NZ, 8, 128), F32),
-            dma((8,)),
+            pltpu.VMEM((NZ, 16, 2048), BF),
             dma((9,)),
             dma((9,)),
-            dma((3, NY)),
-            dma((3, NY)),
+            dma((9,)),
+            dma((4, NY)),
+            dma((4, NY)),
             dma((3, NZ)),
             dma((3, NZ)),
             dma((NDP,)),
@@ -297,10 +296,18 @@
             collective_id=0, has_side_effects=True, vmem_limit_bytes=VMEM_LIMIT
         ),
         name="gather_rows",
-    )(main, over, flag, band)
-
-
-def spread_kernel(slot_ref, pooled_ref, over_ref, am_ref, ao_ref, spot_ref, out_ref, att_ref, rows_ref):
+    )(main, over, flag, band, grad)
+
+
+def spread_kernel(
+    slot_ref, pooled_ref, over_ref, am_ref, ao_ref, spot_ref, wide_ref,
+    out_ref, att_ref, weight_ref,
+    rows_ref,
+):
+    @pl.when(pl.program_id(0) == 0)
+    def _():
+        weight_ref[...] = wide_ref[...].T
+
     slot = slot_ref[...]
     rows = lax.broadcasted_iota(jnp.int32, (2 * MAIN, BYTES), 0)
     onehot = jnp.where(rows == slot, 1.0, 0.0)
@@ -327,7 +334,7 @@
     att_ref[0] = att.astype(BF)
 
 
-def spread(slot, pooled, over, am, ao, spot):
+def spread(slot, pooled, over, am, ao, spot, wide):
     steps = 4
     width = DG // steps
     return pl.pallas_call(
@@ -335,23 +342,26 @@
         grid=(steps,),
         in_specs=[
             pl.BlockSpec((1, BYTES), lambda i: (0, 0)),
-            pl.BlockSpec((72, width), lambda i: (0, i)),
+            pl.BlockSpec((MAIN, width), lambda i: (0, i)),
             pl.BlockSpec((NY, NZ, 2, width), lambda i: (0, 0, 0, i)),
             pl.BlockSpec((1, NZ, 8, 512), lambda i: (i, 0, 0, 0)),
             pl.BlockSpec((1, 8, 512), lambda i: (i, 0, 0)),
             pl.BlockSpec((8, 128), lambda i: (0, 0)),
+            pl.BlockSpec((COLS, HEAD), lambda i: (0, 0)),
         ],
         out_specs=[
             pl.BlockSpec((1, BYTES, width), lambda i: (0, 0, i)),
             pl.BlockSpec((1, 66, 512), lambda i: (0, 0, i)),
+            pl.BlockSpec((HEAD, COLS), lambda i: (0, 0)),
         ],
         out_shape=[
             jax.ShapeDtypeStruct((1, BYTES, DG), BF),
             jax.ShapeDtypeStruct((1, 66, 2048), BF),
+            jax.ShapeDtypeStruct((HEAD, COLS), F32),
         ],
         scratch_shapes=[pltpu.VMEM((2 * MAIN, width), BF)],
         name="spread",
-    )(slot, pooled, over, am, ao, spot)
+    )(slot, pooled, over, am, ao, spot, wide)
 
 
 ROWS = 72
@@ -428,25 +438,24 @@
         target = jnp.where(query, head // 4, lax.rem(head, 4))
         src = proj.at[p, :, i * HEAD : (i + 1) * HEAD]
         dst = heads.at[slot, y]
-        there = send(
+        there = lambda: send(
             src, dst, (hs.at[j, i], hr.at[slot, y]), y=target, x=p // 2, c=lax.rem(p, 2)
         )
-        stay = pltpu.make_async_copy(src, dst, hr.at[slot, y])
-        own = target == y
-        return there, stay, own
+        stay = lambda: pltpu.make_async_copy(src, dst, hr.at[slot, y])
+        return there, stay, target == y
 
     for i in (2, 1, 0):
         for j in range(1, NDP):
-            plan(j, i)[0].start()
+            plan(j, i)[0]().start()
         there, stay, own = plan(0, i)
 
         @pl.when(own)
         def _():
-            stay.start()
+            stay().start()
 
         @pl.when(jnp.logical_not(own))
         def _():
-            there.start()
+            there().start()
 
     def arrived(slot, k):
         pltpu.make_async_copy(heads.at[slot, k], heads.at[slot, k], hr.at[slot, k]).wait()
@@ -484,12 +493,12 @@
         copy.wait()
     for i in range(3):
         for j in range(1, NDP):
-            plan(j, i)[0].wait_send()
+            plan(j, i)[0]().wait_send()
         there, stay, own = plan(0, i)
 
         @pl.when(jnp.logical_not(own))
         def _():
-            there.wait_send()
+            there().wait_send()
 
 
 def to_heads(proj):
@@ -523,13 +532,50 @@
 
 
 def attention_kernel(
-    heads_ref, kv_ref, gy_ref, gz_ref, spot_ref, kidx_ref, qidx_ref, qoidx_ref,
+    heads_ref, kv_ref, gy_ref, gz_ref, spot_ref, owner_ref,
     om_ref, oo_ref, dq_ref, dkv_ref,
-    k_ref, v_ref, kt, vt, g_ref, qo_ref, go_ref, scores, dk, dv,
+    k_ref, v_ref, kt, vt, g_ref, qo_ref, go_ref, scores, dk, dv, kidx_ref, line, qidx_ref, qoidx_ref,
 ):
     chunks = PATCHES // CHUNK
     z = lax.axis_index("z")
-    spot = spot_ref[0:1, 0:1].astype(jnp.int32)
+    spot = spot_ref[0, 0].astype(jnp.int32)
+
+    for t in range(0, PATCHES, 128):
+        w = min(128, PATCHES - t)
+        r = lax.broadcasted_iota(jnp.int32, (w, w), 0)
+        j = lax.broadcasted_iota(jnp.int32, (w, w), 1)
+        own = owner_ref[0:1, t : t + w] == (r & 31)
+        hit = jnp.where(own & ((r >> 5) == (j >> 5)), 1.0, 0.0).astype(BF)
+        down = lax.broadcasted_iota(jnp.int32, (w, 128), 0).astype(F32).astype(BF)
+        along = lax.broadcasted_iota(jnp.int32, (16, w), 1).astype(F32).astype(BF)
+        scores[t : t + w, 0:128] = dot(hit, down) + float(t)
+        line[:, t : t + w] = (
+            lax.dot_general(along, hit, (((1,), (1,)), ((), ())), preferred_element_type=F32)
+            + float(t)
+        )[0:8]
+    row = lax.broadcasted_iota(jnp.int32, (KM, 128), 0)
+    kidx_ref[0:KM, :] = jnp.where(
+        row < MAIN * (spot + 1), scores[0:KM, 0:128], scores[MAIN:PATCHES, 0:128]
+    )
+    base = MAIN * (spot + 1)
+    row = lax.broadcasted_iota(jnp.int32, (MAIN, 128), 0)
+    place = scores[pl.ds(pl.multiple_of(base, MAIN), MAIN), 0:128] - (
+        base + 32 * (row >> 5)
+    ).astype(F32)
+    row = lax.broadcasted_iota(jnp.int32, (MAIN, MAIN), 0)
+    col = lax.broadcasted_iota(jnp.int32, (MAIN, MAIN), 1)
+    mix = jnp.where(col == (row & 1) * 32 + (row >> 1), 1.0, 0.0).astype(BF)
+    place = dot(mix, place.astype(BF))
+    row = lax.broadcasted_iota(jnp.int32, (MAIN, 128), 0)
+    kidx_ref[KM:PATCHES, :] = place + (base + 32 * (row & 1)).astype(F32)
+    window = line[0:1, pl.ds(pl.multiple_of(z * QM, QM), QM + 128)]
+    col = lax.broadcasted_iota(jnp.int32, (1, QM), 1) + z * QM
+    qidx_ref[...] = jnp.where(col < base, window[:, 0:QM], window[:, MAIN : MAIN + QM])
+    row = lax.broadcasted_iota(jnp.int32, (MAIN, QO), 0)
+    col = lax.broadcasted_iota(jnp.int32, (MAIN, QO), 1)
+    mine = jnp.where(row == 8 * z + (col & 7), 1.0, 0.0).astype(BF)
+    col = lax.broadcasted_iota(jnp.int32, (1, QO), 1)
+    qoidx_ref[...] = dot_t(place.astype(BF), mine)[0:1] + (base + 32 * (col & 1)).astype(F32)
 
     for i, ref in enumerate((k_ref, v_ref)):
         for k in range(NZ):
@@ -547,18 +593,15 @@
     late = jnp.where(z * NY + (row >> 6) > spot, 2, 0)
     pick = jnp.where(col == (row & 31) * 16 + (row >> 5) + late, 1.0, 0.0).astype(BF)
     g_ref[...] = dot(pick, gz_ref[...].reshape(512, 512)).astype(BF)
-    row = lax.broadcasted_iota(jnp.int32, (16, 512), 0)
-    col = lax.broadcasted_iota(jnp.int32, (16, 512), 1)
-    group = 2 * spot + 2 + (row & 1)
-    band = jnp.minimum(group >> 3, NZ - 1)
-    pick = jnp.where(
-        (col == (row >> 1) * 128 + band * 16 + group - 8 * band) & (row < 8), 1.0, 0.0
-    ).astype(BF)
-    extra = dot(pick, gy_ref[...].reshape(512, 512)).astype(BF)
-    for h in range(4):
-        go_ref[8 * h : 8 * h + 8, :] = extra[0:8, HEAD * h : HEAD * (h + 1)]
-        for j in range(NY):
-            qo_ref[8 * h + 2 * j : 8 * h + 2 * j + 2, :] = heads_ref[h, j, MAIN : MAIN + 2, :]
+    row = lax.broadcasted_iota(jnp.int32, (16, 66), 0)
+    col = lax.broadcasted_iota(jnp.int32, (16, 66), 1)
+    pick = jnp.where((col == 2 * spot + 2 + row) & (row < 2), 1.0, 0.0).astype(BF)
+    for j in range(NY):
+        extra = dot(pick, gy_ref[j]).astype(BF)
+        for h in range(4):
+            at = 8 * h + 2 * j
+            go_ref[at : at + 2, :] = extra[0:2, HEAD * h : HEAD * (h + 1)]
+            qo_ref[at : at + 2, :] = heads_ref[h, j, MAIN : MAIN + 2, :]
 
     def span(c):
         return pl.ds(pl.multiple_of(c * CHUNK, 32), CHUNK)
@@ -572,7 +615,9 @@
         for c in range(chunks):
             at = span(c)
             s = dot(k_ref[at, :], qt) * FACTOR
-            s = jnp.where(kidx_ref[at, :] <= qidx, s, -jnp.inf)
+            index = kidx_ref[at, :]
+            index = jnp.concatenate([index, index], axis=1) if width > 128 else index[:, :width]
+            s = jnp.where(index <= qidx, s, -jnp.inf)
             scores[at, :width] = s
             peak = jnp.maximum(peak, jnp.max(s, axis=0, keepdims=True))
         total = jnp.zeros((1, width), F32)
@@ -635,10 +680,10 @@
                 dkv_ref[i, k, j, MAIN : MAIN + 2, :] = extra[at : at + 2]
 
 
-def attention(heads, kv, gy, gz, spot, kidx, qidx, qoidx):
+def attention(heads, kv, gy, gz, spot, owner):
     return pl.pallas_call(
         attention_kernel,
-        in_specs=[VM] * 8,
+        in_specs=[VM] * 4 + [pl.BlockSpec(memory_space=pltpu.SMEM), VM],
         out_specs=[VM] * 4,
         out_shape=[
             jax.ShapeDtypeStruct((NS, 8, 512), BF),
@@ -657,17 +702,14 @@
             pltpu.VMEM((PATCHES, QM), F32),
             pltpu.VMEM((PATCHES, HEAD), F32),
             pltpu.VMEM((PATCHES, HEAD), F32),
+            pltpu.VMEM((PATCHES, 128), F32),
+            pltpu.VMEM((8, 2304), F32),
+            pltpu.VMEM((1, QM), F32),
+            pltpu.VMEM((1, QO), F32),
         ],
         compiler_params=pltpu.CompilerParams(vmem_limit_bytes=VMEM_LIMIT),
         name="attention",
-    )(heads, kv, gy, gz, spot, kidx, qidx, qoidx)
-
-
-def add(*parts):
-    total = parts[0].astype(F32)
-    for part in parts[1:]:
-        total = total + part.astype(F32)
-    return total.astype(BF)
+    )(heads, kv, gy, gz, spot, owner)
 
 
 def columns_kernel(
@@ -785,27 +827,33 @@
     )(dq, dkv)
 
 
-def products_kernel(main_ref, over_ref, cols_ref, weight_ref, part_ref, back_ref, cm, co, over_rows):
+def products_kernel(
+    main_ref, over_ref, cols_ref, weight_ref,
+    part_ref, back_ref, extra_ref,
+    cm, co, cmt, cot, over_rows,
+):
     @pl.when(pl.program_id(0) == 0)
     def _():
         for n in range(NDP):
             cm[MAIN * n : MAIN * (n + 1), :] = cols_ref[n, 0:MAIN, :]
             co[2 * n : 2 * n + 2, :] = cols_ref[n, MAIN : MAIN + 2, :]
+        cmt[...] = cm[...].astype(F32).T.astype(BF)
+        cot[...] = co[...].astype(F32).T.astype(BF)
 
     width = weight_ref.shape[0]
     for n in range(NDP):
         over_rows[2 * n : 2 * n + 2, :] = over_ref[n]
-    part = dot_t(main_ref[...].reshape(NDP * MAIN, width), cm[...]) + dot_t(over_rows[...], co[...])
-    part_ref[0] = part.astype(BF).reshape(NY, HEAD, COLS)
+    part = dot(cmt[...], main_ref[...].reshape(NDP * MAIN, width)) + dot(cot[...], over_rows[...])
+    part = part.astype(BF)
+    for k in range(NY):
+        part_ref[0, k] = part[:, HEAD * k : HEAD * (k + 1)]
     turn = (((1,), (1,)), ((), ()))
     back = lax.dot_general(cm[...], weight_ref[...], turn, preferred_element_type=F32)
+    back_ref[...] = back.astype(BF).reshape(NDP, MAIN, width)
     extra = lax.dot_general(co[...], weight_ref[...], turn, preferred_element_type=F32)
-    back = back.astype(BF)
     extra = extra.astype(BF)
     for n in range(NDP):
-        back_ref[n, 0:MAIN, :] = back[MAIN * n : MAIN * (n + 1)]
-        back_ref[n, MAIN:ROWS, :] = jnp.zeros((ROWS - MAIN, width), BF)
-        back_ref[n, MAIN : MAIN + 2, :] = extra[2 * n : 2 * n + 2]
+        extra_ref[n] = extra[2 * n : 2 * n + 2]
 
 
 def products(all_main, all_over, cols, weight):
@@ -821,16 +869,20 @@
             pl.BlockSpec((width, COLS), lambda i: (i, 0)),
         ],
         out_specs=[
-            pl.BlockSpec((1, NY, HEAD, COLS), lambda i: (i, 0, 0, 0)),
-            pl.BlockSpec((NDP, ROWS, width), lambda i: (0, 0, i)),
+            pl.BlockSpec((1, NY, COLS, HEAD), lambda i: (i, 0, 0, 0)),
+            pl.BlockSpec((NDP, MAIN, width), lambda i: (0, 0, i)),
+            pl.BlockSpec((NDP, 2, width), lambda i: (0, 0, i)),
         ],
         out_shape=[
-            jax.ShapeDtypeStruct((NZ, NY, HEAD, COLS), BF),
-            jax.ShapeDtypeStruct((NDP, ROWS, DG), BF),
+            jax.ShapeDtypeStruct((NZ, NY, COLS, HEAD), BF),
+            jax.ShapeDtypeStruct((NDP, MAIN, DG), BF),
+            jax.ShapeDtypeStruct((NDP, 2, DG), BF),
         ],
         scratch_shapes=[
             pltpu.VMEM((NDP * MAIN, COLS), BF),
             pltpu.VMEM((16, COLS), BF),
+            pltpu.VMEM((COLS, NDP * MAIN), BF),
+            pltpu.VMEM((COLS, 16), BF),
             pltpu.VMEM((16, width), BF),
         ],
         compiler_params=pltpu.CompilerParams(vmem_limit_bytes=VMEM_LIMIT),
@@ -838,25 +890,31 @@
     )(all_main, all_over, cols, weight)
 
 
+LONG = 256
+SHORT = COLS - LONG
+
+
 def sums_kernel(
-    back, w, om, oo,
+    back, extra, w, om, oo,
     pooled, over_all, wgrad, am, ao,
     own, sib, chip, xa, xb, xr, xl, sxa, sxb,
-    ya, yb, yr, yl, sa, sb, wy, ubuf, usum, dbuf, dsum, omz, ov, oz,
-    local, cs, cr, xs, xrv, ws, wr, us, ur, ds, dr, zs, zr, os_, or_,
+    ya, yb, yr, yl, sa, sb, wy, wz, ubuf, usum, dbuf, dsum, wb, wq, obuf, omz, ov, oz,
+    local, cs, cr, xs, xrv, ws, wr, us, ur, ds, dr, zs, zr, os_, or_, ps, pr,
 ):
     z, y, x, c = here()
+    n = x * 2 + c
     right, left, far = lax.rem(x + 1, NX), lax.rem(x + 3, NX), lax.rem(x + 2, NX)
     yn, yp, yf = lax.rem(y + 1, NY), lax.rem(y + 3, NY), lax.rem(y + 2, NY)
     up, down = lax.rem(z + 1, NZ), lax.rem(z + NZ - 1, NZ)
     ys_at = [lax.rem(y + j, NY) for j in range(NY)]
     zs_at = [lax.rem(z + j, NZ) for j in range(NZ)]
+    dp_at = [lax.rem(n + j, NDP) for j in range(NDP)]
     greet(
         [{"y": ys_at[j]} for j in range(1, NY)]
         + [{"z": zs_at[j]} for j in range(1, NZ)]
-        + [{"x": right}, {"x": left}, {"c": 1 - c}]
+        + [{"x": p // 2, "c": lax.rem(p, 2)} for p in dp_at[1:]]
     )
-    copies = []
+    copies, stays = [], []
 
     def go(src, dst, pair, **device):
         copy = send(src, dst, pair, **device)
@@ -864,34 +922,67 @@
         copies.append(copy)
         return copy
 
+    def stay(src, dst):
+        copy = pltpu.make_async_copy(src, dst, local.at[len(stays)])
+        copy.start()
+        stays.append(copy)
+        return copy
+
+    waited = []
+
+    def done(copy):
+        copy.wait()
+        waited.append(copy)
+
+    def at(k):
+        return lax.rem(z + k, NZ)
+
     order = (far, right, left, x)
     halves = [
         go(back.at[p * 2 + 1 - c], sib.at[p], (cs.at[k], cr.at[k]), c=1 - c)
         for k, p in enumerate(order)
     ]
-    loads = [
-        pltpu.make_async_copy(back.at[p * 2 + c], own.at[p], local.at[k])
-        for k, p in enumerate(order)
+    loads = [stay(back.at[p * 2 + c], own.at[p]) for p in order]
+
+    overs = [
+        go(extra.at[p], obuf.at[n], (ps.at[j], pr.at[j]), x=p // 2, c=lax.rem(p, 2))
+        for j, p in enumerate(dp_at)
+        if j
     ]
-    for copy in loads:
-        copy.start()
-
+    here_o = stay(extra.at[n], obuf.at[n])
+
+    short, long = pl.ds(LONG, SHORT), pl.ds(0, LONG)
+    ups, downs = {}, {}
+
+    def ring(t):
+        for i in range(2):
+            some = pl.ds(2 * i, 2)
+            if t == 1:
+                above, below = w.at[at(4), some, short], w.at[at(5), some, short]
+            else:
+                ups[t - 1, i].wait_recv()
+                usum[t - 2, i] = add(ubuf[t - 2, i], w[at(5 - t), some, short])
+                above = usum.at[t - 2, i]
+                if t < 4:
+                    downs[t - 1, i].wait_recv()
+                    dsum[t - 2, i] = add(dbuf[t - 2, i], w[at(4 + t), some, short])
+                    below = dsum.at[t - 2, i]
+            ups[t, i] = go(above, ubuf.at[t - 1, i], (us.at[t - 1, i], ur.at[t - 1, i]), z=up)
+            if t < 4:
+                downs[t, i] = go(
+                    below, dbuf.at[t - 1, i], (ds.at[t - 1, i], dr.at[t - 1, i]), z=down
+                )
+
+    ring(1)
     lo, hi = pl.ds(0, 4), pl.ds(4, 4)
-    w_a = go(w.at[lo, yf], ya, (ws.at[0], wr.at[0]), y=yn)
-    w_b = go(w.at[hi, yf], yb, (ws.at[1], wr.at[1]), y=yp)
-    w_hi = go(w.at[hi, yn], yr.at[hi], (ws.at[2], wr.at[2]), y=yn)
-    w_lo = go(w.at[lo, yp], yl.at[lo], (ws.at[3], wr.at[3]), y=yp)
-
-    rows_z = [
-        go(om.at[zs_at[j]], omz.at[z], (zs.at[0, j], zr.at[0, j]), z=zs_at[j])
-        for j in range(1, NZ)
-    ]
-    stay_z = pltpu.make_async_copy(om.at[z], omz.at[z], local.at[4])
-    stay_z.start()
+    w_a = go(w.at[lo, yf, long], ya, (ws.at[0], wr.at[0]), y=yn)
+    w_b = go(w.at[hi, yf, long], yb, (ws.at[1], wr.at[1]), y=yp)
+    w_hi = go(w.at[hi, yn, long], yr.at[hi], (ws.at[2], wr.at[2]), y=yn)
+    w_lo = go(w.at[lo, yp, long], yl.at[lo], (ws.at[3], wr.at[3]), y=yp)
 
     first, second = pl.ds(0, DG // 2), pl.ds(DG // 2, DG // 2)
     for k, p in enumerate(order):
-        loads[k].wait()
+        done(loads[k])
         halves[k].wait_recv()
         chip[p] = add(own[p], sib[p])
         if k == 0:
@@ -902,101 +993,106 @@
         if k == 2:
             x_lo = go(chip.at[p, :, first], xl.at[:, first], (xs.at[3], xrv.at[3]), x=left)
 
+    for copy in overs:
+        copy.wait_recv()
+    done(here_o)
+    ov[...] = add(*[obuf[k] for k in range(NDP)])
+    over_z = [go(ov, oz.at[z], (zs.at[1, j], zr.at[1, j]), z=zs_at[j]) for j in range(1, NZ)]
+    keep_oz = stay(ov, oz.at[z])
+    ring(2)
     w_a.wait_recv()
-    sa[...] = add(ya[...], w[lo, yn])
+    sa[...] = add(ya[...], w[lo, yn, long])
     w_lo2 = go(sa, yr.at[lo], (ws.at[4], wr.at[4]), y=yn)
     w_b.wait_recv()
-    sb[...] = add(yb[...], w[hi, yp])
+    sb[...] = add(yb[...], w[hi, yp, long])
     w_hi2 = go(sb, yl.at[hi], (ws.at[5], wr.at[5]), y=yp)
+    ring(3)
     x_a.wait_recv()
     sxa[...] = add(xa[...], chip[right, :, first])
     x_lo2 = go(sxa, xr.at[:, first], (xs.at[4], xrv.at[4]), x=right)
     x_b.wait_recv()
     sxb[...] = add(xb[...], chip[left, :, second])
     x_hi2 = go(sxb, xl.at[:, second], (xs.at[5], xrv.at[5]), x=left)
+    for copy in over_z:
+        copy.wait_recv()
+    done(keep_oz)
+    over_y = [
+        go(oz, over_all.at[y], (os_.at[2, j], or_.at[2, j]), y=ys_at[j]) for j in range(1, NY)
+    ]
+    stay(oz, over_all.at[y])
+    ring(4)
+    rows_z = [
+        go(om.at[zs_at[j]], omz.at[z], (zs.at[0, j], zr.at[0, j]), z=zs_at[j])
+        for j in range(1, NZ)
+    ]
+    here_z = stay(om.at[z], omz.at[z])
+
+    for copy in (w_hi, w_lo, w_lo2, w_hi2):
+        copy.wait_recv()
+    wy[...] = add(w[:, y, long], yr[...], yl[...])
+    longs = [
+        go(wy.at[zs_at[j]], wz.at[j], (zs.at[2, j], zr.at[2, j]), z=zs_at[j])
+        for j in range(1, NZ)
+    ]
+    for i in range(2):
+        downs[3, i].wait_recv()
+        ups[4, i].wait_recv()
+        some = pl.ds(2 * i, 2)
+        wb[some] = add(w[z, some, short], ubuf[3, i], dbuf[2, i])
+    shorts = [
+        go(wb.at[ys_at[j]], wq.at[j], (os_.at[3, j], or_.at[3, j]), y=ys_at[j])
+        for j in range(1, NY)
+    ]
 
     for copy in rows_z:
         copy.wait_recv()
-    stay_z.wait()
+    done(here_z)
     rows_y = []
     for j in range(1, NY):
         k = ys_at[j]
         rows_y.append(go(omz.at[:, k], am.at[y], (os_.at[0, j], or_.at[0, j]), y=k))
         rows_y.append(go(oo.at[k], ao.at[y], (os_.at[1, j], or_.at[1, j]), y=k))
-    stay_y = [
-        pltpu.make_async_copy(omz.at[:, y], am.at[y], local.at[5]),
-        pltpu.make_async_copy(oo.at[y], ao.at[y], local.at[6]),
-    ]
-    for copy in stay_y:
-        copy.start()
+    stay(omz.at[:, y], am.at[y])
+    stay(oo.at[y], ao.at[y])
 
     for copy in (x_hi, x_lo, x_lo2, x_hi2):
         copy.wait_recv()
     pooled[...] = add(chip[x], xr[...], xl[...])
-    ov[...] = pooled[MAIN : MAIN + 2, :]
-    over_z = [
-        go(ov, oz.at[z], (zs.at[1, j], zr.at[1, j]), z=zs_at[j]) for j in range(1, NZ)
-    ]
-    keep_z = pltpu.make_async_copy(ov, oz.at[z], local.at[7])
-    keep_z.start()
-
-    for copy in (w_hi, w_lo, w_lo2, w_hi2):
+    for copy in shorts:
         copy.wait_recv()
-    wy[...] = add(w[:, y], yr[...], yl[...])
-
-    def at(k):
-        return lax.rem(z + k, NZ)
-
-    ups, downs = {}, {}
-    over_y = []
-    for t in range(1, 5):
-        if t == 1:
-            above, below = wy.at[at(4)], wy.at[at(5)]
-        else:
-            ups[t - 1].wait_recv()
-            usum[t - 2] = add(ubuf[t - 2], wy[at(5 - t)])
-            above = usum.at[t - 2]
-            if t < 4:
-                downs[t - 1].wait_recv()
-                dsum[t - 2] = add(dbuf[t - 2], wy[at(4 + t)])
-                below = dsum.at[t - 2]
-        ups[t] = go(above, ubuf.at[t - 1], (us.at[t - 1], ur.at[t - 1]), z=up)
-        if t < 4:
-            downs[t] = go(below, dbuf.at[t - 1], (ds.at[t - 1], dr.at[t - 1]), z=down)
-        if t == 1:
-            for copy in over_z:
-                copy.wait_recv()
-            keep_z.wait()
-            for j in range(1, NY):
-                over_y.append(
-                    go(oz, over_all.at[y], (os_.at[2, j], or_.at[2, j]), y=ys_at[j])
-                )
-            keep_y = pltpu.make_async_copy(oz, over_all.at[y], local.at[8])
-            keep_y.start()
-    downs[3].wait_recv()
-    ups[4].wait_recv()
-    wgrad[...] = ubuf[3].astype(F32) + dbuf[2].astype(F32) + wy[z].astype(F32)
+    total = wb[y].astype(F32)
+    for j in range(1, NY):
+        total = total + wq[j].astype(F32)
+    wgrad[short, :] = total
+    for copy in longs:
+        copy.wait_recv()
+    total = wy[z].astype(F32)
+    for j in range(1, NZ):
+        total = total + wz[j].astype(F32)
+    wgrad[long, :] = total
     for copy in (*over_y, *rows_y):
         copy.wait_recv()
     for copy in copies:
         copy.wait_send()
-    for copy in (*stay_y, keep_y):
-        copy.wait()
-
-
-def sums(back, part, om, oo):
+    for copy in stays:
+        if not any(copy is other for other in waited):
+            copy.wait()
+
+
+def sums(back, extra, part, om, oo):
     dma = pltpu.SemaphoreType.DMA
-    rows = (ROWS, DG)
-    half = (ROWS, DG // 2)
-    block = (HEAD, COLS)
+    rows = (MAIN, DG)
+    half = (MAIN, DG // 2)
+    long = (LONG, HEAD)
+    short = (2, SHORT, HEAD)
     return pl.pallas_call(
         sums_kernel,
-        in_specs=[ANY, VM, ANY, ANY],
+        in_specs=[ANY, ANY, VM, ANY, ANY],
         out_specs=[VM, ANY, VM, ANY, ANY],
         out_shape=[
             jax.ShapeDtypeStruct(rows, BF),
             jax.ShapeDtypeStruct((NY, NZ, 2, DG), BF),
-            jax.ShapeDtypeStruct(block, F32),
+            jax.ShapeDtypeStruct((COLS, HEAD), F32),
             jax.ShapeDtypeStruct((NY, NZ, 8, 512), BF),
             jax.ShapeDtypeStruct((NY, 8, 512), BF),
         ],
@@ -1005,74 +1101,59 @@
             *[pltpu.VMEM(half, BF)] * 2,
             *[pltpu.VMEM(rows, BF)] * 2,
             *[pltpu.VMEM(half, BF)] * 2,
-            *[pltpu.VMEM((4, *block), BF)] * 2,
-            *[pltpu.VMEM((8, *block), BF)] * 2,
-            *[pltpu.VMEM((4, *block), BF)] * 2,
-            pltpu.VMEM((8, *block), BF),
-            pltpu.VMEM((4, *block), BF),
-            pltpu.VMEM((3, *block), BF),
-            pltpu.VMEM((3, *block), BF),
-            pltpu.VMEM((2, *block), BF),
+            *[pltpu.VMEM((4, *long), BF)] * 2,
+            *[pltpu.VMEM((8, *long), BF)] * 2,
+            *[pltpu.VMEM((4, *long), BF)] * 2,
+            *[pltpu.VMEM((8, *long), BF)] * 2,
+            pltpu.VMEM((4, 2, *short), BF),
+            pltpu.VMEM((3, 2, *short), BF),
+            pltpu.VMEM((3, 2, *short), BF),
+            pltpu.VMEM((2, 2, *short), BF),
+            pltpu.VMEM((4, SHORT, HEAD), BF),
+            pltpu.VMEM((4, SHORT, HEAD), BF),
+            pltpu.VMEM((NDP, 2, DG), BF),
             pltpu.VMEM((NZ, NY, 8, 512), BF),
             pltpu.VMEM((2, DG), BF),
             pltpu.VMEM((NZ, 2, DG), BF),
-            dma((9,)),
+            dma((10,)),
             dma((4,)),
             dma((4,)),
             dma((6,)),
             dma((6,)),
             dma((6,)),
             dma((6,)),
-            dma((4,)),
-            dma((4,)),
-            dma((3,)),
-            dma((3,)),
-            dma((2, NZ)),
-            dma((2, NZ)),
-            dma((3, NY)),
-            dma((3, NY)),
+            dma((4, 2)),
+            dma((4, 2)),
+            dma((3, 2)),
+            dma((3, 2)),
+            dma((3, NZ)),
+            dma((3, NZ)),
+            dma((4, NY)),
+            dma((4, NY)),
+            dma((NDP,)),
+            dma((NDP,)),
         ],
         compiler_params=pltpu.CompilerParams(
             collective_id=3, has_side_effects=True, vmem_limit_bytes=VMEM_LIMIT
         ),
         name="sums",
-    )(back, part, om, oo)
+    )(back, extra, part, om, oo)
 
 
 def body(byte_states, byte_patch, patch_owner, qkv_weight, attention_output_gradient):
-    z, y = lax.axis_index("z"), lax.axis_index("y")
-    s = z * NY + y
     main, over, slot, flag, band = pool(
         byte_patch, patch_owner, byte_states, attention_output_gradient
     )
-    all_main, all_over, found, grad_y, grad_z = gather_rows(main, over, flag, band)
-    spot = found[0, 0].astype(jnp.int32)
-
-    owners = patch_owner[0].reshape(66, 32)
-    who = jnp.arange(32, dtype=jnp.int32)
-    place = jnp.sum(
-        jnp.where(owners[:, :, None] == who[None, None, :], who[None, :, None], 0), axis=1
+    all_main, all_over, spot, gy, gz = gather_rows(
+        main, over, flag, band, attention_output_gradient
     )
-    index = place + 32 * jnp.arange(66, dtype=jnp.int32)[:, None]
-    flat = index.reshape(-1)
-    row = jnp.arange(2048, dtype=jnp.int32)
-    main_index = jnp.where(row < MAIN * (spot + 1), flat[:2048], flat[64:])
-    over_index = lax.dynamic_slice_in_dim(index, 2 * spot + 2, 2, 0).T.reshape(-1)
-    key_index = jnp.concatenate([main_index, over_index])
-    query_index = lax.dynamic_slice_in_dim(main_index, z * QM, QM)
-    query_over_index = lax.dynamic_slice_in_dim(over_index, z * 8, 8)
-
-    proj = project(all_main, all_over, qkv_weight)
-    heads, kv = to_heads(proj)
-    om, oo, dq, dkv = attention(
-        heads, kv, grad_y, grad_z, found,
-        key_index[:, None], query_index[None], jnp.tile(query_over_index, 4)[None],
-    )
-
+    heads, kv = to_heads(project(all_main, all_over, qkv_weight))
+    om, oo, dq, dkv = attention(heads, kv, gy, gz, spot, patch_owner)
     cols = to_columns(dq, dkv)
-    part, back = products(all_main, all_over, cols, qkv_weight)
-    pooled, over_back, weight_grad, am, ao = sums(back, part, om.reshape(NZ, NY, 8, 512), oo)
-    state_grad, att = spread(slot, pooled, over_back, am, ao, found)
+    part, back, extra = products(all_main, all_over, cols, qkv_weight)
+    om = om.reshape(NZ, NY, 8, 512)
+    pooled, over_back, wide, am, ao = sums(back, extra, part, om, oo)
+    state_grad, att, weight_grad = spread(slot, pooled, over_back, am, ao, spot, wide)
     return att, state_grad, weight_grad
 
 

time: 214 us -> 191 us (0.89)
  Pallas kernels: 204 us -> 190 us
  local copies, waits for them, and re-layouts: 6.21 us -> 0 us
    pallas_call x3, Pallas kernels: 116 us -> 102 us  [the longest x1 46.6 us: sums(): pl.pallas_call(sums_kernel, in_specs=[ANY, ANY, VM, ANY, ANY], out_specs=...]
where the time goes in v2:
time: 191 us
  Pallas kernels  190 us (99%)
    pallas_call x1, Pallas kernels, sums(): pl.pallas_call(sums_kernel, in_specs=[ANY, ANY, VM, ANY, ANY], out_specs=...  46.6 us
    pallas_call x1, Pallas kernels, gather_rows(): pl.pallas_call(gather_kernel, in_specs=[ANY, ANY, VM, ANY, ANY], out_spec...  36.3 us
    pallas_call x1, Pallas kernels, to_columns(): pl.pallas_call(columns_kernel, in_specs=[VM, VM], out_specs=ANY, out_shap...  31.3 us
    pallas_call x1, Pallas kernels, to_heads(): pl.pallas_call(heads_kernel, in_specs=[ANY], out_specs=[ANY, ANY], out_sh...  30.4 us
    pallas_call x1, Pallas kernels, attention(): pl.pallas_call(attention_kernel, in_specs=[VM] * 4 + [pl.BlockSpec(memory...  19.2 us
    pallas_call x1, Pallas kernels, products(): pl.pallas_call(products_kernel, grid=(steps,), in_specs=[pl.BlockSpec((ND...  10.5 us
    pallas_call x1, Pallas kernels, project(): pl.pallas_call(project_kernel, grid=(steps,), in_specs=[pl.BlockSpec((NDP...  6.31 us
    pallas_call x1, Pallas kernels, spread(): pl.pallas_call(spread_kernel, grid=(steps,), in_specs=[pl.BlockSpec((1, B...  4.84 us

profile of v2, /device:TPU:6, one launch (start us, length us, event | category | flops | bytes accessed | tf_op | source)
XLA Modules:
  0.0 190.5 jit_solution(11713795408195188135)
XLA Ops:
  0.6 4.4 %pool.1 = (bf16[64,4096]{1,0:T(8,128)(2,1)}, bf16[4,16,4096]{2,1,0:T(8,128)(2,1)}, s32[1,256]{1,0:T(1,128)}, f32[8,128]{1,0:T(8,128)}, bf16[8,16,2048]{2,1,0:T(8,128)(2,1)}) custom-call(s32[1,256]{1,0:T(1,128)} %ids_ref.1, s32[1,2112]{1,0:T(1,128)} %owner_ref.3, bf16[1,256,4096]{2,1,0:T(8,128)(2,1)} %states_ref.1, bf16[1,66,2048]{2,1,0:T(8,128)(2,1)} %grad.1), custom_call_target="tpu_custom_call" | custom-call | tf_op jit(solution)/shard_map/pool/pallas_call | solution.py:77
  5.1 36.3 %gather_rows.1 = (bf16[8,64,4096]{2,1,0:T(8,128)(2,1)}, bf16[8,2,4096]{2,1,0:T(2,128)(2,1)}, f32[8,128]{1,0:T(8,128)}, bf16[4,66,512]{2,1,0:T(8,128)(2,1)}, bf16[8,4,16,512]{3,2,1,0:T(8,128)(2,1)}) custom-call(bf16[64,4096]{1,0:T(8,128)(2,1)} %get-tuple-element.31.main, bf16[4,16,4096]{2,1,0:T(8,128)(2,1)} %get-tuple-element.32.over, ...), custom_call_target="tpu_custom_call" | custom-call | tf_op jit(solution)/shard_map/gather_rows/pallas_call | solution.py:265
  41.4 6.3 %project.1.proj = bf16[8,72,384]{2,1,0:T(8,128)(2,1)} custom-call(bf16[8,64,4096]{2,1,0:T(8,128)(2,1)} %get-tuple-element.35.main_ref, bf16[8,2,4096]{2,1,0:T(2,128)(2,1)} %get-tuple-element.36.over_ref, bf16[4096,384]{1,0:T(8,128)(2,1)} %weight_ref.3), custom_call_target="tpu_custom_call" | custom-call | tf_op jit(solution)/shard_map/project/pallas_call | solution.py:398
  47.7 30.4 %to_heads.1 = (bf16[6,4,72,128]{3,2,1,0:T(8,128)(2,1)}, bf16[2,8,4,72,128]{4,3,2,1,0:T(8,128)(2,1)}) custom-call(bf16[8,72,384]{2,1,0:T(8,128)(2,1)} %project.1.proj), custom_call_target="tpu_custom_call" | custom-call | tf_op jit(solution)/shard_map/to_heads/pallas_call | solution.py:506
  78.1 19.2 %attention.1 = (bf16[32,8,512]{2,1,0:T(8,128)(2,1)}, bf16[4,8,512]{2,1,0:T(8,128)(2,1)}, bf16[4,4,72,128]{3,2,1,0:T(8,128)(2,1)}, bf16[2,8,4,72,128]{4,3,2,1,0:T(8,128)(2,1)}) custom-call(bf16[6,4,72,128]{3,2,1,0:T(8,128)(2,1)} %get-tuple-element.37.heads_ref, bf16[2,8,4,72,128]{4,3,2,1,0:T(8,128)(2,1)} %get-tuple-element.38.kv_ref, ...), custom_call_target="tpu_custom_call" | custom-call | tf_op jit(solution)/shard_map/attention/pallas_call | solution.py:684
  97.3 31.3 %to_columns.1.cols_ref = bf16[8,72,384]{2,1,0:T(8,128)(2,1)} custom-call(bf16[4,4,72,128]{3,2,1,0:T(8,128)(2,1)} %get-tuple-element.42.dq, bf16[2,8,4,72,128]{4,3,2,1,0:T(8,128)(2,1)} %get-tuple-element.43.dkv), custom_call_target="tpu_custom_call" | custom-call | tf_op jit(solution)/shard_map/to_columns/pallas_call | solution.py:805
  128.6 10.5 %products.1 = (bf16[8,4,384,128]{3,2,1,0:T(8,128)(2,1)}, bf16[8,64,4096]{2,1,0:T(8,128)(2,1)}, bf16[8,2,4096]{2,1,0:T(2,128)(2,1)}) custom-call(bf16[8,64,4096]{2,1,0:T(8,128)(2,1)} %get-tuple-element.35.main_ref, bf16[8,2,4096]{2,1,0:T(2,128)(2,1)} %get-tuple-element.36.over_ref, bf16[8,72,384]{2,1,0:T(8,128)(2,1)} %to_columns.1.cols_ref, ...), custom_call_target="tpu_custom_call" | custom-call | tf_op jit(solution)/shard_map/products/pallas_call | solution.py:862
  139.1 46.6 %sums.1 = (bf16[64,4096]{1,0:T(8,128)(2,1)}, bf16[4,8,2,4096]{3,2,1,0:T(2,128)(2,1)}, f32[384,128]{1,0:T(8,128)}, bf16[4,8,8,512]{3,2,1,0:T(8,128)(2,1)}, bf16[4,8,512]{2,1,0:T(8,128)(2,1)}) custom-call(bf16[8,64,4096]{2,1,0:T(8,128)(2,1)} %get-tuple-element.44.back, bf16[8,2,4096]{2,1,0:T(2,128)(2,1)} %get-tuple-element.45.extra, ...), custom_call_target="tpu_custom_call" | custom-call | tf_op jit(solution)/shard_map/sums/pallas_call | solution.py:1088
  185.7 4.8 %spread.1 = (bf16[1,256,4096]{2,1,0:T(8,128)(2,1)}, bf16[1,66,2048]{2,1,0:T(8,128)(2,1)}, f32[128,384]{1,0:T(8,128)}) custom-call(s32[1,256]{1,0:T(1,128)} %get-tuple-element.30.slot_ref, bf16[64,4096]{1,0:T(8,128)(2,1)} %get-tuple-element.49.pooled_ref, bf16[4,8,2,4096]{3,2,1,0:T(2,128)(2,1)} %get-tuple-element.50.over_ref, ...), custom_call_target="tpu_custom_call" | custom-call | tf_op jit(solution)/shard_map/spread/pallas_call | solution.py:340

commit v3 on v2

--- a/solution.py
+++ b/solution.py
@@ -108,6 +108,8 @@
 
 
 def add(*parts):
+    if len(parts) == 2:
+        return parts[0] + parts[1]
     total = parts[0].astype(F32)
     for part in parts[1:]:
         total = total + part.astype(F32)
@@ -130,173 +132,6 @@
     for device in devices:
         pl.semaphore_signal(barrier, inc=1, device_id=device, device_id_type=MESH)
     pl.semaphore_wait(barrier, len(devices))
-
-
-def gather_kernel(
-    main, over, flag, band, grad,
-    all_main, all_over, spot, gy, gz,
-    ybuf, zsrc, zbuf, mine, fy, fsum, fz, gband,
-    local, main_s, main_r, ys, yr, zs, zr, os_, or_,
-):
-    z, y, x, c = here()
-    n = x * 2 + c
-    ys_at = [lax.rem(y + j, NY) for j in range(NY)]
-    zs_at = [lax.rem(z + j, NZ) for j in range(NZ)]
-    dp_at = [lax.rem(n + j, NDP) for j in range(NDP)]
-    right, left, twin = lax.rem(x + 1, NX), lax.rem(x + 3, NX), 1 - c
-    greet(
-        [{"y": ys_at[j]} for j in range(1, NY)]
-        + [{"z": zs_at[j]} for j in range(1, NZ)]
-        + [{"x": p // 2, "c": lax.rem(p, 2)} for p in dp_at[1:]]
-    )
-    copies, stays = [], []
-
-    def go(src, dst, pair, **device):
-        copy = send(src, dst, pair, **device)
-        copy.start()
-        copies.append(copy)
-        return copy
-
-    def stay(src, dst):
-        copy = pltpu.make_async_copy(src, dst, local.at[len(stays)])
-        copy.start()
-        stays.append(copy)
-        return copy
-
-    def half(block, i):
-        return block.at[pl.ds(32 * i, 32), :]
-
-    def pair(i):
-        return main_s.at[i], main_r.at[i]
-
-    def columns(h):
-        return pl.ds(pl.multiple_of(h * 512, 512), 512)
-
-    stage_y = []
-    for j in range(1, NY):
-        k = ys_at[j]
-        stage_y.append(go(over.at[k], ybuf.at[y], (ys.at[0, j], yr.at[0, j]), y=k))
-        stage_y.append(go(flag, fy.at[y], (ys.at[1, j], yr.at[1, j]), y=k))
-    here_y = [stay(over.at[y], ybuf.at[y]), stay(flag, fy.at[y])]
-
-    mine_out = all_main.at[n]
-    to_right = go(main, mine_out, pair(1), x=right)
-    to_left = go(main, mine_out, pair(2), x=left)
-    to_other = go(main, mine_out, pair(0), c=twin)
-    stay(main, mine_out)
-
-    bands_z = [
-        go(band.at[zs_at[j]], gband.at[z], (zs.at[2, j], zr.at[2, j]), z=zs_at[j])
-        for j in range(1, NZ)
-    ]
-    here_band = stay(band.at[z], gband.at[z])
-
-    for copy in stage_y:
-        copy.wait_recv()
-    for copy in here_y:
-        copy.wait()
-    rows = add(ybuf[0], ybuf[1], ybuf[2], ybuf[3])
-    for k in range(NZ):
-        zsrc[k] = rows[2 * k : 2 * k + 2]
-    fsum[...] = fy[0] + fy[1] + fy[2] + fy[3]
-    stage_z = []
-    for j in range(1, NZ):
-        k = zs_at[j]
-        stage_z.append(go(zsrc.at[k], zbuf.at[z], (zs.at[0, j], zr.at[0, j]), z=k))
-        stage_z.append(go(fsum, fz.at[z], (zs.at[1, j], zr.at[1, j]), z=k))
-    here_z = [stay(zsrc.at[z], zbuf.at[z]), stay(fsum, fz.at[z])]
-    grads_y = [
-        go(grad.at[0, :, columns(ys_at[j])], gy.at[y], (ys.at[2, j], yr.at[2, j]), y=ys_at[j])
-        for j in range(1, NY)
-    ]
-    stay(grad.at[0, :, columns(y)], gy.at[y])
-
-    for copy in stage_z:
-        copy.wait_recv()
-    for copy in here_z:
-        copy.wait()
-    total = zbuf[0].astype(F32)
-    found = fz[0]
-    for k in range(1, NZ):
-        total = total + zbuf[k].astype(F32)
-        found = found + fz[k]
-    mine[...] = total.astype(BF)
-    spot[...] = found
-    overs = [
-        go(mine, all_over.at[n], (os_.at[j], or_.at[j]), x=dp_at[j] // 2, c=lax.rem(dp_at[j], 2))
-        for j in range(1, NDP)
-    ]
-    stay(mine, all_over.at[n])
-
-    from_left = all_main.at[left * 2 + c]
-    from_right = all_main.at[right * 2 + c]
-    far = all_main.at[lax.rem(x + 2, NX) * 2 + c]
-    to_right.wait_recv()
-    on_right = go(half(from_left, 0), half(from_left, 0), pair(3), x=right)
-    side_left = go(from_left, from_left, pair(5), c=twin)
-    to_left.wait_recv()
-    on_left = go(half(from_right, 1), half(from_right, 1), pair(4), x=left)
-    side_right = go(from_right, from_right, pair(6), c=twin)
-
-    for copy in bands_z:
-        copy.wait_recv()
-    here_band.wait()
-    bands_y = [
-        go(gband.at[:, :, columns(ys_at[j])], gz.at[:, y], (ys.at[3, j], yr.at[3, j]), y=ys_at[j])
-        for j in range(1, NY)
-    ]
-    stay(gband.at[:, :, columns(y)], gz.at[:, y])
-
-    on_right.wait_recv()
-    side_a = go(half(far, 0), half(far, 0), pair(7), c=twin)
-    on_left.wait_recv()
-    side_b = go(half(far, 1), half(far, 1), pair(8), c=twin)
-    for copy in (to_other, side_left, side_right, side_a, side_b, *overs, *grads_y, *bands_y):
-        copy.wait_recv()
-    for copy in copies:
-        copy.wait_send()
-    for copy in stays:
-        if not any(copy is other for other in (*here_y, *here_z, here_band)):
-            copy.wait()
-
-
-def gather_rows(main, over, flag, band, grad):
-    dma = pltpu.SemaphoreType.DMA
-    return pl.pallas_call(
-        gather_kernel,
-        in_specs=[ANY, ANY, VM, ANY, ANY],
-        out_specs=[ANY, ANY, VM, ANY, ANY],
-        out_shape=[
-            jax.ShapeDtypeStruct((NDP, MAIN, DG), BF),
-            jax.ShapeDtypeStruct((NDP, 2, DG), BF),
-            jax.ShapeDtypeStruct((8, 128), F32),
-            jax.ShapeDtypeStruct((NY, 66, 512), BF),
-            jax.ShapeDtypeStruct((NZ, NY, 16, 512), BF),
-        ],
-        scratch_shapes=[
-            pltpu.VMEM((NY, 16, DG), BF),
-            pltpu.VMEM((NZ, 2, DG), BF),
-            pltpu.VMEM((NZ, 2, DG), BF),
-            pltpu.VMEM((2, DG), BF),
-            pltpu.VMEM((NY, 8, 128), F32),
-            pltpu.VMEM((8, 128), F32),
-            pltpu.VMEM((NZ, 8, 128), F32),
-            pltpu.VMEM((NZ, 16, 2048), BF),
-            dma((9,)),
-            dma((9,)),
-            dma((9,)),
-            dma((4, NY)),
-            dma((4, NY)),
-            dma((3, NZ)),
-            dma((3, NZ)),
-            dma((NDP,)),
-            dma((NDP,)),
-        ],
-        compiler_params=pltpu.CompilerParams(
-            collective_id=0, has_side_effects=True, vmem_limit_bytes=VMEM_LIMIT
-        ),
-        name="gather_rows",
-    )(main, over, flag, band, grad)
 
 
 def spread_kernel(
@@ -365,164 +200,311 @@
 
 
 ROWS = 72
-OVER = 2
-
-
-def project_kernel(main_ref, over_ref, weight_ref, out_ref, acc, acc_over, over_rows):
-    step = pl.program_id(0)
-
-    @pl.when(step == 0)
-    def _():
-        acc[...] = jnp.zeros_like(acc)
-        acc_over[...] = jnp.zeros_like(acc_over)
-
-    for n in range(NDP):
-        over_rows[2 * n : 2 * n + 2, :] = over_ref[n]
-    weight = weight_ref[...]
-    acc[...] += dot(main_ref[...].reshape(NDP * MAIN, weight.shape[0]), weight)
-    acc_over[...] += dot(over_rows[...], weight)
-
-    @pl.when(step == pl.num_programs(0) - 1)
-    def _():
-        total = acc[...].astype(BF)
-        extra = acc_over[...].astype(BF)
-        for n in range(NDP):
-            out_ref[n, 0:MAIN, :] = total[MAIN * n : MAIN * (n + 1)]
-            out_ref[n, MAIN:ROWS, :] = jnp.zeros((ROWS - MAIN, COLS), BF)
-            out_ref[n, MAIN : MAIN + 2, :] = extra[2 * n : 2 * n + 2]
-
-
-def project(all_main, all_over, weight):
-    steps = 4
-    depth = DG // steps
-    return pl.pallas_call(
-        project_kernel,
-        grid=(steps,),
-        in_specs=[
-            pl.BlockSpec((NDP, MAIN, depth), lambda i: (0, 0, i)),
-            pl.BlockSpec((NDP, 2, depth), lambda i: (0, 0, i)),
-            pl.BlockSpec((depth, COLS), lambda i: (i, 0)),
-        ],
-        out_specs=pl.BlockSpec((NDP, ROWS, COLS), lambda i: (0, 0, 0)),
-        out_shape=jax.ShapeDtypeStruct((NDP, ROWS, COLS), BF),
-        scratch_shapes=[
-            pltpu.VMEM((NDP * MAIN, COLS), F32),
-            pltpu.VMEM((16, COLS), F32),
-            pltpu.VMEM((16, depth), BF),
-        ],
-        compiler_params=pltpu.CompilerParams(vmem_limit_bytes=VMEM_LIMIT),
-        name="project",
-    )(all_main, all_over, weight)
 
 
 def lanes(i):
     return pl.ds(pl.multiple_of(i * HEAD, HEAD), HEAD)
 
 
-def heads_kernel(proj, heads, kv, local, hs, hr, rs, rr, ls, lr):
+def front_kernel(
+    main, over, flag, band, grad, weight,
+    all_main, all_over, spot, gy, gz, heads, kv,
+    rows, wide, extras, extra_rows, proj, ybuf, zsrc, zbuf, mine, fy, fsum, fz, gband,
+    local, main_s, main_r, ys, yr, zs, zr, os_, or_, hs, hr, rs, rr, ls, lr,
+):
     z, y, x, c = here()
     n = x * 2 + c
-    up, down = lax.rem(z + 1, NZ), lax.rem(z + NZ - 1, NZ)
-    peers = []
-    for j in range(NDP * NY):
-        if j:
-            p, q = lax.rem(n + j // NY, NDP), lax.rem(y + j, NY)
-            peers.append({"y": q, "x": p // 2, "c": lax.rem(p, 2)})
-    greet(peers + [{"z": up}, {"z": down}])
-
-    def plan(j, i):
-        p = lax.rem(n + j, NDP)
+    ys_at = [lax.rem(y + j, NY) for j in range(NY)]
+    zs_at = [lax.rem(z + j, NZ) for j in range(NZ)]
+    xs_at = [lax.rem(x + j, NX) for j in range(NX)]
+    right, left, twin = xs_at[1], xs_at[3], 1 - c
+    up, down = zs_at[1], zs_at[7]
+    deals = [(d, e) for d in range(NX) for e in range(2)]
+    core = [c, twin]
+    greet(
+        [
+            {"y": ys_at[j], "x": xs_at[d], "c": core[e]}
+            for d, e in deals
+            for j in range(NY)
+            if d or e or j
+        ]
+        + [{"z": zs_at[j]} for j in range(1, NZ)]
+    )
+    copies, stays, waited = [], [], []
+
+    def go(src, dst, pair, **device):
+        copy = send(src, dst, pair, **device)
+        copy.start()
+        copies.append(copy)
+        return copy
+
+    def stay(src, dst):
+        copy = pltpu.make_async_copy(src, dst, local.at[len(stays)])
+        copy.start()
+        stays.append(copy)
+        return copy
+
+    def done(copy):
+        copy.wait()
+        waited.append(copy)
+
+    def half(block, i):
+        return block.at[pl.ds(32 * i, 32), :]
+
+    def pair(i):
+        return main_s.at[i], main_r.at[i]
+
+    def columns(h):
+        return pl.ds(pl.multiple_of(h * 512, 512), 512)
+
+    stage_y = []
+    for j in range(1, NY):
+        k = ys_at[j]
+        stage_y.append(go(over.at[k], ybuf.at[y], (ys.at[0, j], yr.at[0, j]), y=k))
+        stage_y.append(go(flag, fy.at[y], (ys.at[1, j], yr.at[1, j]), y=k))
+    here_y = [stay(over.at[y], ybuf.at[y]), stay(flag, fy.at[y])]
+
+    block = rows.at[n]
+    right_a = go(half(main, 0), half(block, 0), pair(1), x=right)
+    left_b = go(half(main, 1), half(block, 1), pair(2), x=left)
+    right_b = go(half(main, 1), half(block, 1), pair(3), x=right)
+    left_a = go(half(main, 0), half(block, 0), pair(4), x=left)
+    to_twin = go(main, block, pair(0), c=twin)
+    stay(main, all_main.at[n])
+    here_w = stay(weight, wide)
+
+    bands_z = [
+        go(band.at[zs_at[j]], gband.at[z], (zs.at[2, j], zr.at[2, j]), z=zs_at[j])
+        for j in range(1, NZ)
+    ]
+    here_band = stay(band.at[z], gband.at[z])
+
+    for copy in stage_y:
+        copy.wait_recv()
+    for copy in here_y:
+        done(copy)
+    summed = add(ybuf[0], ybuf[1], ybuf[2], ybuf[3])
+    for k in range(NZ):
+        zsrc[k] = summed[2 * k : 2 * k + 2]
+    fsum[...] = fy[0] + fy[1] + fy[2] + fy[3]
+    stage_z = []
+    for j in range(1, NZ):
+        k = zs_at[j]
+        stage_z.append(go(zsrc.at[k], zbuf.at[z], (zs.at[0, j], zr.at[0, j]), z=k))
+        stage_z.append(go(fsum, fz.at[z], (zs.at[1, j], zr.at[1, j]), z=k))
+    here_z = [stay(zsrc.at[z], zbuf.at[z]), stay(fsum, fz.at[z])]
+    grads_y = [
+        go(grad.at[0, :, columns(ys_at[j])], gy.at[y], (ys.at[2, j], yr.at[2, j]), y=ys_at[j])
+        for j in range(1, NY)
+    ]
+    stay(grad.at[0, :, columns(y)], gy.at[y])
+
+    def seq(d, e):
+        return xs_at[d] * 2 + core[e]
+
+    def project(blocks, tail=None):
+        parts = [value for _, value in blocks] + ([] if tail is None else [tail])
+        product = dot(jnp.concatenate(parts, axis=0), wide[...]).astype(BF)
+        for k, (place, _) in enumerate(blocks):
+            proj[place, 0:MAIN, :] = product[MAIN * k : MAIN * (k + 1)]
+        return product[MAIN * len(blocks) :]
+
+    done(here_w)
+    to_twin.wait_recv()
+    project([(n, main[...]), (seq(0, 1), rows[seq(0, 1)])])
+    proj[:, MAIN:ROWS, :] = jnp.zeros((NDP, ROWS - MAIN, COLS), BF)
+
+    for copy in stage_z:
+        copy.wait_recv()
+    for copy in here_z:
+        done(copy)
+    total = zbuf[0].astype(F32)
+    found = fz[0]
+    for k in range(1, NZ):
+        total = total + zbuf[k].astype(F32)
+        found = found + fz[k]
+    mine[...] = total.astype(BF)
+    spot[...] = found
+    overs = [
+        go(mine, extras.at[n], (os_.at[2 * d + e], or_.at[2 * d + e]), x=xs_at[d], c=core[e])
+        for d, e in deals
+        if d or e
+    ]
+    here_o = stay(mine, extras.at[n])
+
+    from_left, from_right = rows.at[left * 2 + c], rows.at[right * 2 + c]
+    far = rows.at[xs_at[2] * 2 + c]
+    right_a.wait_recv()
+    on_right = go(half(from_left, 0), half(from_left, 0), pair(5), x=right)
+    left_b.wait_recv()
+    on_left = go(half(from_right, 1), half(from_right, 1), pair(6), x=left)
+    right_b.wait_recv()
+    side_left = go(from_left, from_left, pair(7), c=twin)
+    left_a.wait_recv()
+    side_right = go(from_right, from_right, pair(8), c=twin)
+
+    for copy in bands_z:
+        copy.wait_recv()
+    done(here_band)
+    bands_y = [
+        go(gband.at[:, :, columns(ys_at[j])], gz.at[:, y], (ys.at[3, j], yr.at[3, j]), y=ys_at[j])
+        for j in range(1, NY)
+    ]
+    stay(gband.at[:, :, columns(y)], gz.at[:, y])
+
+    for copy in overs:
+        copy.wait_recv()
+    done(here_o)
+    for p in range(NDP):
+        extra_rows[2 * p : 2 * p + 2, :] = extras[p]
+    stay(extras, all_over)
+    side_left.wait_recv()
+    side_right.wait_recv()
+    near = [seq(1, 0), seq(3, 0), seq(1, 1), seq(3, 1)]
+    tail = project([(p, rows[p]) for p in near], extra_rows[...])
+    for p in range(NDP):
+        proj[p, MAIN : MAIN + 2, :] = tail[2 * p : 2 * p + 2]
+
+    def plan(d, e, i):
         head = n * 3 + i
         query = head < QUERY_HEADS
         slot = jnp.where(query, lax.rem(head, 4), head // 4)
         target = jnp.where(query, head // 4, lax.rem(head, 4))
-        src = proj.at[p, :, i * HEAD : (i + 1) * HEAD]
+        src = proj.at[seq(d, e), :, i * HEAD : (i + 1) * HEAD]
         dst = heads.at[slot, y]
         there = lambda: send(
-            src, dst, (hs.at[j, i], hr.at[slot, y]), y=target, x=p // 2, c=lax.rem(p, 2)
+            src, dst, (hs.at[2 * d + e, i], hr.at[slot, y]), y=target, x=xs_at[d], c=core[e]
         )
-        stay = lambda: pltpu.make_async_copy(src, dst, hr.at[slot, y])
-        return there, stay, target == y
-
-    for i in (2, 1, 0):
-        for j in range(1, NDP):
-            plan(j, i)[0]().start()
-        there, stay, own = plan(0, i)
-
-        @pl.when(own)
-        def _():
-            stay().start()
-
-        @pl.when(jnp.logical_not(own))
-        def _():
-            there().start()
+        here_ = lambda: pltpu.make_async_copy(src, dst, hr.at[slot, y])
+        return there, here_, target == y
+
+    def scatter(d, e):
+        for i in (2, 1, 0):
+            there, here_, own = plan(d, e, i)
+            if d or e:
+                there().start()
+            else:
+
+                @pl.when(own)
+                def _():
+                    here_().start()
+
+                @pl.when(jnp.logical_not(own))
+                def _():
+                    there().start()
+
+    for d in (1, 3, 0):
+        for e in range(2):
+            scatter(d, e)
+    on_right.wait_recv()
+    side_a = go(half(far, 0), half(far, 0), pair(9), c=twin)
+    on_left.wait_recv()
+    side_b = go(half(far, 1), half(far, 1), pair(10), c=twin)
+    side_a.wait_recv()
+    side_b.wait_recv()
+    project([(seq(2, e), rows[seq(2, e)]) for e in range(2)])
+    for e in range(2):
+        scatter(2, e)
+    for d, e in deals:
+        if d or e:
+            stay(rows.at[seq(d, e)], all_main.at[seq(d, e)])
 
     def arrived(slot, k):
         pltpu.make_async_copy(heads.at[slot, k], heads.at[slot, k], hr.at[slot, k]).wait()
 
-    ups, downs, keeps = [], [], []
+    ups, downs = {}, {}
     for t in range(1, 5):
         for i in range(2):
+            above_at, below_at = lax.rem(z + NZ - (t - 1), NZ), lax.rem(z + (t - 1), NZ)
             if t == 1:
                 for k in range(NY):
                     arrived(4 + i, k)
-                keep = pltpu.make_async_copy(heads.at[4 + i], kv.at[i, z], local.at[i])
-                keep.start()
-                keeps.append(keep)
+                stay(heads.at[4 + i], kv.at[i, z])
                 above = below = heads.at[4 + i]
             else:
-                ups[2 * (t - 2) + i].wait_recv()
-                downs[2 * (t - 2) + i].wait_recv()
-                above = kv.at[i, lax.rem(z + NZ - (t - 1), NZ)]
-                below = kv.at[i, lax.rem(z + (t - 1), NZ)]
-            copy = send(above, kv.at[i, lax.rem(z + NZ - (t - 1), NZ)], (rs.at[t - 1, i], rr.at[t - 1, i]), z=up)
-            copy.start()
-            ups.append(copy)
-            if t < 4:
-                copy = send(below, kv.at[i, lax.rem(z + (t - 1), NZ)], (ls.at[t - 1, i], lr.at[t - 1, i]), z=down)
-                copy.start()
-                downs.append(copy)
+                ups[t - 1, i].wait_recv()
+                downs[t - 1, i].wait_recv()
+                above, below = kv.at[i, above_at], kv.at[i, below_at]
+            if t < 4 or i == 0:
+                ups[t, i] = go(
+                    above, kv.at[i, above_at], (rs.at[t - 1, i], rr.at[t - 1, i]), z=up
+                )
+            if t < 4 or i == 1:
+                downs[t, i] = go(
+                    below, kv.at[i, below_at], (ls.at[t - 1, i], lr.at[t - 1, i]), z=down
+                )
     for slot in range(4):
         for k in range(NY):
             arrived(slot, k)
-    for i in range(2):
-        ups[6 + i].wait_recv()
-    for copy in ups + downs:
+    for copy in (ups[4, 0], downs[4, 1], *grads_y, *bands_y):
+        copy.wait_recv()
+    for copy in copies:
         copy.wait_send()
-    for copy in keeps:
-        copy.wait()
-    for i in range(3):
-        for j in range(1, NDP):
-            plan(j, i)[0]().wait_send()
-        there, stay, own = plan(0, i)
-
-        @pl.when(jnp.logical_not(own))
-        def _():
-            there().wait_send()
-
-
-def to_heads(proj):
+    for copy in stays:
+        if not any(copy is other for other in waited):
+            copy.wait()
+    for d, e in deals:
+        for i in range(3):
+            there, _, own = plan(d, e, i)
+            if d or e:
+                there().wait_send()
+            else:
+
+                @pl.when(jnp.logical_not(own))
+                def _():
+                    there().wait_send()
+
+
+def front(main, over, flag, band, grad, weight):
     dma = pltpu.SemaphoreType.DMA
     return pl.pallas_call(
-        heads_kernel,
-        in_specs=[ANY],
-        out_specs=[ANY, ANY],
+        front_kernel,
+        in_specs=[VM] * 5 + [ANY],
+        out_specs=[ANY, ANY, VM, VM, ANY, VM, ANY],
         out_shape=[
+            jax.ShapeDtypeStruct((NDP, MAIN, DG), BF),
+            jax.ShapeDtypeStruct((NDP, 2, DG), BF),
+            jax.ShapeDtypeStruct((8, 128), F32),
+            jax.ShapeDtypeStruct((NY, 66, 512), BF),
+            jax.ShapeDtypeStruct((NZ, NY, 16, 512), BF),
             jax.ShapeDtypeStruct((6, NY, ROWS, HEAD), BF),
             jax.ShapeDtypeStruct((2, NZ, NY, ROWS, HEAD), BF),
         ],
         scratch_shapes=[
-            dma((2,)),
+            pltpu.VMEM((NDP, MAIN, DG), BF),
+            pltpu.VMEM((DG, COLS), BF),
+            pltpu.VMEM((NDP, 2, DG), BF),
+            pltpu.VMEM((16, DG), BF),
+            pltpu.VMEM((NDP, ROWS, COLS), BF),
+            pltpu.VMEM((NY, 16, DG), BF),
+            pltpu.VMEM((NZ, 2, DG), BF),
+            pltpu.VMEM((NZ, 2, DG), BF),
+            pltpu.VMEM((2, DG), BF),
+            pltpu.VMEM((NY, 8, 128), F32),
+            pltpu.VMEM((8, 128), F32),
+            pltpu.VMEM((NZ, 8, 128), F32),
+            pltpu.VMEM((NZ, 16, 2048), BF),
+            dma((20,)),
+            dma((11,)),
+            dma((11,)),
+            dma((4, NY)),
+            dma((4, NY)),
+            dma((3, NZ)),
+            dma((3, NZ)),
+            dma((NDP,)),
+            dma((NDP,)),
             dma((NDP, 3)),
             dma((6, NY)),
             dma((4, 2)),
             dma((4, 2)),
-            dma((3, 2)),
-            dma((3, 2)),
-        ],
-        compiler_params=pltpu.CompilerParams(collective_id=1, has_side_effects=True),
-        name="to_heads",
-    )(proj)
+            dma((4, 2)),
+            dma((4, 2)),
+        ],
+        compiler_params=pltpu.CompilerParams(
+            collective_id=0, has_side_effects=True, vmem_limit_bytes=VMEM_LIMIT
+        ),
+        name="front",
+    )(main, over, flag, band, grad, weight)
 
 
 CHUNK = 352
@@ -1087,8 +1069,8 @@
     short = (2, SHORT, HEAD)
     return pl.pallas_call(
         sums_kernel,
-        in_specs=[ANY, ANY, VM, ANY, ANY],
-        out_specs=[VM, ANY, VM, ANY, ANY],
+        in_specs=[ANY, ANY, VM, VM, VM],
+        out_specs=[VM, ANY, VM, ANY, VM],
         out_shape=[
             jax.ShapeDtypeStruct(rows, BF),
             jax.ShapeDtypeStruct((NY, NZ, 2, DG), BF),
@@ -1144,10 +1126,9 @@
     main, over, slot, flag, band = pool(
         byte_patch, patch_owner, byte_states, attention_output_gradient
     )
-    all_main, all_over, spot, gy, gz = gather_rows(
-        main, over, flag, band, attention_output_gradient
+    all_main, all_over, spot, gy, gz, heads, kv = front(
+        main, over, flag, band, attention_output_gradient, qkv_weight
     )
-    heads, kv = to_heads(project(all_main, all_over, qkv_weight))
     om, oo, dq, dkv = attention(heads, kv, gy, gz, spot, patch_owner)
     cols = to_columns(dq, dkv)
     part, back, extra = products(all_main, all_over, cols, qkv_weight)

time: 191 us -> 181 us (0.948)
  Pallas kernels: 190 us -> 179 us
    pallas_call x4 -> x2, Pallas kernels: 120 us -> 107 us  [the longest x1 60.9 us: front(): pl.pallas_call(front_kernel, in_specs=[VM] * 5 + [ANY], out_specs=[ANY, A...]
where the time goes in v3:
time: 181 us; the launch traced here: 180 us
  Pallas kernels  179 us (99%)
    pallas_call x1, Pallas kernels, front(): pl.pallas_call(front_kernel, in_specs=[VM] * 5 + [ANY], out_specs=[ANY, A...  60.9 us
    pallas_call x1, Pallas kernels, sums(): pl.pallas_call(sums_kernel, in_specs=[ANY, ANY, VM, VM, VM], out_specs=[V...  46.2 us
    pallas_call x1, Pallas kernels, to_columns(): pl.pallas_call(columns_kernel, in_specs=[VM, VM], out_specs=ANY, out_shap...  33.1 us
    pallas_call x1, Pallas kernels, attention(): pl.pallas_call(attention_kernel, in_specs=[VM] * 4 + [pl.BlockSpec(memory...  19.2 us
    pallas_call x1, Pallas kernels, products(): pl.pallas_call(products_kernel, grid=(steps,), in_specs=[pl.BlockSpec((ND...  10.5 us
    pallas_call x1, Pallas kernels, spread(): pl.pallas_call(spread_kernel, grid=(steps,), in_specs=[pl.BlockSpec((1, B...  4.85 us
    pallas_call x1, Pallas kernels, pool(): pl.pallas_call(pool_kernel, grid=(steps,), in_specs=[pl.BlockSpec((1, BYT...  4.39 us

profile of v3, /device:TPU:6, one launch (start us, length us, event | category | flops | bytes accessed | tf_op | source)
XLA Modules:
  0.0 179.8 jit_solution(950814003801321883)
XLA Ops:
  0.6 4.4 %pool.1 = (bf16[64,4096]{1,0:T(8,128)(2,1)}, bf16[4,16,4096]{2,1,0:T(8,128)(2,1)}, s32[1,256]{1,0:T(1,128)}, f32[8,128]{1,0:T(8,128)}, bf16[8,16,2048]{2,1,0:T(8,128)(2,1)}) custom-call(s32[1,256]{1,0:T(1,128)} %ids_ref.1, s32[1,2112]{1,0:T(1,128)} %owner_ref.3, bf16[1,256,4096]{2,1,0:T(8,128)(2,1)} %states_ref.1, bf16[1,66,2048]{2,1,0:T(8,128)(2,1)} %grad.1), custom_call_target="tpu_custom_call" | custom-call | tf_op jit(solution)/shard_map/pool/pallas_call | solution.py:77
  5.0 60.9 %front.1 = (bf16[8,64,4096]{2,1,0:T(8,128)(2,1)}, bf16[8,2,4096]{2,1,0:T(2,128)(2,1)}, f32[8,128]{1,0:T(8,128)}, bf16[4,66,512]{2,1,0:T(8,128)(2,1)}, bf16[8,4,1...) custom-call(bf16[64,4096]{1,0:T(8,128)(2,1)} %get-tuple-element.31.main, ...), custom_call_target="tpu_custom_call" | custom-call | tf_op jit(solution)/shard_map/front/pallas_call | solution.py:460
  66.0 19.2 %attention.1 = (bf16[32,8,512]{2,1,0:T(8,128)(2,1)}, bf16[4,8,512]{2,1,0:T(8,128)(2,1)}, bf16[4,4,72,128]{3,2,1,0:T(8,128)(2,1)}, bf16[2,8,4,72,128]{4,3,2,1,0:T(8,128)(2,1)}) custom-call(bf16[6,4,72,128]{3,2,1,0:T(8,128)(2,1)} %get-tuple-element.37.heads_ref, bf16[2,8,4,72,128]{4,3,2,1,0:T(8,128)(2,1)} %get-tuple-element.38.kv_ref, ...), custom_call_target="tpu_custom_call" | custom-call | tf_op jit(solution)/shard_map/attention/pallas_call | solution.py:666
  85.2 33.1 %to_columns.1.cols_ref = bf16[8,72,384]{2,1,0:T(8,128)(2,1)} custom-call(bf16[4,4,72,128]{3,2,1,0:T(8,128)(2,1)} %get-tuple-element.42.dq, bf16[2,8,4,72,128]{4,3,2,1,0:T(8,128)(2,1)} %get-tuple-element.43.dkv), custom_call_target="tpu_custom_call" | custom-call | tf_op jit(solution)/shard_map/to_columns/pallas_call | solution.py:787
  118.3 10.5 %products.1 = (bf16[8,4,384,128]{3,2,1,0:T(8,128)(2,1)}, bf16[8,64,4096]{2,1,0:T(8,128)(2,1)}, bf16[8,2,4096]{2,1,0:T(2,128)(2,1)}) custom-call(bf16[8,64,4096]{2,1,0:T(8,128)(2,1)} %get-tuple-element.35.main_ref, bf16[8,2,4096]{2,1,0:T(2,128)(2,1)} %get-tuple-element.36.over_ref, bf16[8,72,384]{2,1,0:T(8,128)(2,1)} %to_columns.1.cols_ref, ...), custom_call_target="tpu_custom_call" | custom-call | tf_op jit(solution)/shard_map/products/pallas_call | solution.py:844
  128.8 46.2 %sums.1 = (bf16[64,4096]{1,0:T(8,128)(2,1)}, bf16[4,8,2,4096]{3,2,1,0:T(2,128)(2,1)}, f32[384,128]{1,0:T(8,128)}, bf16[4,8,8,512]{3,2,1,0:T(8,128)(2,1)}, bf16[4,8,512]{2,1,0:T(8,128)(2,1)}) custom-call(bf16[8,64,4096]{2,1,0:T(8,128)(2,1)} %get-tuple-element.44.back, bf16[8,2,4096]{2,1,0:T(2,128)(2,1)} %get-tuple-element.45.extra, ...), custom_call_target="tpu_custom_call" | custom-call | tf_op jit(solution)/shard_map/sums/pallas_call | solution.py:1070
  174.9 4.8 %spread.1 = (bf16[1,256,4096]{2,1,0:T(8,128)(2,1)}, bf16[1,66,2048]{2,1,0:T(8,128)(2,1)}, f32[128,384]{1,0:T(8,128)}) custom-call(s32[1,256]{1,0:T(1,128)} %get-tuple-element.30.slot_ref, bf16[64,4096]{1,0:T(8,128)(2,1)} %get-tuple-element.49.pooled_ref, bf16[4,8,2,4096]{3,2,1,0:T(2,128)(2,1)} %get-tuple-element.50.over_ref, ...), custom_call_target="tpu_custom_call" | custom-call | tf_op jit(solution)/shard_map/spread/pallas_call | solution.py:175
